TPU v7x, 256 devices: a whole 4x4x8 slice. The times are simulated.
256 devices in a mesh: dp: 4 (over z_hi, core), ctx: 16 (over z_lo, y), tp: 4 (over x).
Axes of the slice: x: 4, y: 4, z: 8 (z_hi: 2, z_lo: 4; z = z_hi * 4 + z_lo), core: 2. Of those that a mesh axis runs over, the one named last changes fastest.
Arguments:
- teacher_part: bfloat16 [4, 4, 4096, 8192], P('dp', 'tp', 'ctx'), may hold values from -8 to 8
- student_in: bfloat16 [4, 4096, 4096], P('dp', 'ctx'), may hold values from -24 to 24
- out_proj: bfloat16 [4096, 4096], P('ctx', 'tp'), may hold values from -0.09375 to 0.09375
- segment_ids: int32 [4, 4096], P('dp'), may hold values from 0 to 7, never falling along the last dimension, each value on 1 to 1024 neighbouring positions
- valid_count: int32 [4], P('dp'), may hold values from 256 to 4096, as said below
Outputs:
- doc_loss: float32 [4], P('dp')
- wo_grad: float32 [4096, 4096], P('ctx', 'tp')
- state_grad: float32 [4, 4096, 4096], P('dp', 'ctx', 'tp')
Inputs may be any that keep to these rules, and one draw needn't show every extreme that they name: `valid_count`: one document in every draw is valid at all 4096 positions. `segment_ids`: segment numbers never fall along a document.
All inputs are finite; a program needn't handle non-finite values.
Results may differ from a plain program's by a relative error of at most 0.019.
The roundings to bfloat16 on the way count: a program that leaves them out, or rounds other values in their place, can miss the bound.
Values may be sent and summed in bfloat16 or wider, within the bound.
A program may use at most 64 MiB of HBM per device.

v0:
```python
import math

import jax
import jax.numpy as jnp
from jax import lax
from jax.sharding import PartitionSpec as P

DS = 4096
HEADS = 32


masked_score = -1e30


def shifted_2(value, axis, steps):
    count = lax.axis_size(axis)
    leading, last = (max(0, -steps), min(count, count - steps))
    return lax.ppermute(value, axis, [(source, source + steps) for source in range(leading, last)])


def log_probs(scores, allowed):
    scores = jnp.where(allowed[None, :, :], scores, masked_score)
    top = jnp.max(scores, axis=-1, keepdims=True)
    shifted = scores - top
    return shifted - jnp.log(jnp.sum(jnp.exp(shifted), axis=-1, keepdims=True))


def window_terms(
    teacher_query, teacher_keys, student_query, student_keys, allowed, live, head_count
):
    length = teacher_query.shape[0]
    teacher_qh = teacher_query.reshape(length, head_count, -1)
    teacher_kh = teacher_keys.reshape(2 * length, head_count, -1)
    student_qh = student_query.reshape(length, head_count, -1)
    student_kh = student_keys.reshape(2 * length, head_count, -1)
    teacher_scale = 1.0 / math.sqrt(teacher_qh.shape[-1])
    student_scale = 1.0 / math.sqrt(student_qh.shape[-1])
    teacher_scores = (
        jnp.einsum("qhd,khd->hqk", teacher_qh, teacher_kh, preferred_element_type=jnp.float32)
        * teacher_scale
    )
    student_scores = (
        jnp.einsum("qhd,khd->hqk", student_qh, student_kh, preferred_element_type=jnp.float32)
        * student_scale
    )
    teacher_logp = log_probs(teacher_scores, allowed)
    student_logp = log_probs(student_scores, allowed)
    teacher_prob = jnp.exp(teacher_logp)
    student_prob = jnp.exp(student_logp)
    divergence = jnp.sum(teacher_prob * (teacher_logp - student_logp), axis=-1)
    loss_part = jnp.sum(divergence * live[None, :]) / HEADS
    grad_scale = live[None, :, None] * (student_scale / HEADS)
    score_grad = ((student_prob - teacher_prob) * grad_scale).astype(jnp.bfloat16)
    query_grad = jnp.einsum(
        "hqk,khd->qhd", score_grad, student_kh, preferred_element_type=jnp.float32
    ).reshape(length, -1)
    key_grad = jnp.einsum(
        "hqk,qhd->khd", score_grad, student_qh, preferred_element_type=jnp.float32
    ).reshape(2 * length, -1)
    return (loss_part, query_grad, key_grad)


def per_device(teacher_part, student_in, out_proj, segment_ids, valid_count):
    window_len = student_in.shape[1]
    head_count = HEADS // lax.axis_size("tp")
    unscale = HEADS * math.sqrt(DS // HEADS)
    partial_sum = teacher_part[0, 0].astype(jnp.float32)
    teacher_own = lax.psum_scatter(
        partial_sum.astype(jnp.bfloat16), "tp", scatter_dimension=1, tiled=True
    )
    tokens = student_in[0]
    columns = tokens
    student_own = jnp.dot(
        columns,
        lax.all_gather(out_proj, "ctx", axis=0, tiled=True),
        preferred_element_type=jnp.float32,
    ).astype(jnp.bfloat16)
    teacher_prev, student_prev = shifted_2((teacher_own, student_own), "ctx", 1)
    teacher_keys = jnp.concatenate([teacher_prev, teacher_own], 0)
    student_keys = jnp.concatenate([student_prev, student_own], 0)
    window = lax.axis_index("ctx")
    start = window * window_len
    segments = segment_ids[0]
    segment_padded = jnp.concatenate([jnp.full((window_len,), -1, jnp.int32), segments], 0)
    query_segment = lax.dynamic_slice_in_dim(segments, start, window_len, 0)
    key_segment = lax.dynamic_slice_in_dim(segment_padded, start, 2 * window_len, 0)
    valid_limit = valid_count[0]
    query_position = start + jnp.arange(window_len, dtype=jnp.int32)
    key_position = start - window_len + jnp.arange(2 * window_len, dtype=jnp.int32)
    allowed = (key_segment[None, :] == query_segment[:, None]) & (
        key_position[None, :] < valid_limit
    )
    live = jnp.where(query_position < valid_limit, 1.0, 0.0).astype(jnp.float32)
    loss_part, query_grad, key_grad = window_terms(
        teacher_own, teacher_keys, student_own, student_keys, allowed, live, head_count
    )
    from_next = shifted_2(key_grad[:window_len].astype(jnp.bfloat16), "ctx", -1).astype(jnp.float32)
    hidden_grad = (query_grad + key_grad[window_len:] + from_next).astype(jnp.bfloat16)
    state_grad = (hidden_grad.astype(jnp.float32) * unscale)[None]
    columns = tokens
    grad_piece = lax.psum_scatter(
        jnp.einsum("tr,tc->rc", columns, hidden_grad, preferred_element_type=jnp.float32).astype(
            jnp.bfloat16
        ),
        "ctx",
        scatter_dimension=0,
        tiled=True,
    )
    wo_grad = lax.psum(grad_piece, "dp").astype(jnp.float32)
    doc_loss = lax.psum(loss_part, ("ctx", "tp"))
    return (doc_loss.reshape(1), wo_grad, state_grad)


def solution(mesh):
    return jax.shard_map(
        per_device,
        mesh=mesh,
        in_specs=(
            P("dp", "tp", "ctx", None),
            P("dp", "ctx", None),
            P("ctx", "tp"),
            P("dp", None),
            P("dp"),
        ),
        out_specs=(P("dp"), P("ctx", "tp"), P("dp", "ctx", "tp")),
        check_vma=False,
    )
```

profile of v0, /device:TPU:0, one launch (start us, length us, event | category | flops | bytes accessed | tf_op | source)
XLA Modules:
  0.0 515.2 jit_solution(8294521861776870635)
XLA Ops:
  8.1 6.5 %copy.32 = bf16[1,1,256,8192]{2,3,1,0:T(8,128)(2,1)} copy(bf16[1,1,256,8192]{3,2,1,0:T(8,128)(2,1)} %param.5) | data formatting | bytes 8388608 | tf_op args[0]
  14.6 0.5 all-gather.2.cloned.1.call-update
  15.2 50.1 %reduce-scatter.3.cloned.1.call-done = bf16[256,2048]{0,1:T(8,128)(2,1)} async-done(((bf16[256,8192]{0,1:T(8,128)(2,1)}), bf16[256,2048]{0,1:T(8,128)(2,1)}) %reduce-scatter.3.cloned.1.call-update) | async-done | bytes 1048592 | tf_op jit(solution)/shard_map/reduce_scatter | solution.py:68
  65.4 3.5 collective-permute-start
  69.6 0.2 compare_and_fusion
  69.8 44.8 %collective-permute-done = bf16[256,2048]{0,1:T(8,128)(2,1)S(1)} collective-permute-done((bf16[256,2048]{0,1:T(8,128)(2,1)}, bf16[256,2048]{0,1:T(8,128)(2,1)S(1)}, u32[]{:S(2)}, u32[]{:S(2)}) %collective-permute-start) | collective-permute-done | bytes 1048608 | tf_op jit(solution)/shard_map/ppermute | solution.py:18
  114.6 2.8 pad_maximum_fusion
  117.4 23.7 %all-gather.2.cloned.1.call-done = bf16[4096,1024]{1,0:T(8,128)(2,1)} async-done(((bf16[256,1024]{1,0:T(8,128)(2,1)}), bf16[4096,1024]{1,0:T(8,128)(2,1)}) %all-gather.2.cloned.1.call-update) | async-done | bytes 8388624 | tf_op jit(solution)/shard_map/all_gather | solution.py:75
  141.2 5.7 %fusion.24 = bf16[256,1024]{1,0:T(8,128)(2,1)S(1)} fusion(bf16[4096,1024]{1,0:T(8,128)(2,1)} %all-gather.2.cloned.1.call-done, bf16[1,256,4096]{2,1,0:T(8,128)(2,1)S(1)} %copy-done), kind=kOutput, calls=%fused_computation.32 | convolution fusion | flops 2147745792 | bytes 11010048 | tf_op jit(solution)/shard_map/dot_general | solution.py:73
  146.9 3.1 collective-permute-start.1
  150.0 5.2 %fusion.8 = f32[8,256,512]{1,2,0:T(8,128)} fusion(pred[256,512]{0,1:T(8,128)(4,1)S(1)} %compare_and_fusion, bf16[512,8,256]{0,2,1:T(8,128)(2,1)} %bitcast.58, bf16[256,8,256]{0,2,1:T(8,128)(2,1)} %bitcast.60), kind=kOutput, calls=%fused_computation.17 | convolution fusion | flops 540019200 | bytes 7471104 | tf_op jit(solution)/shard_map/sub | solution.py:24
  155.2 6.2 %log_subtract_fusion.1 = f32[8,256,512]{1,2,0:T(8,128)} fusion(f32[8,256,512]{1,2,0:T(8,128)} %fusion.8), kind=kOutput, calls=%fused_computation.6 | output fusion | flops 1051135 | bytes 8388608 | tf_op jit(solution)/shard_map/reduce_sum | solution.py:25
  161.4 1.0 copy.50
  162.4 1.0 pad_maximum_fusion.1
  163.4 1.5 copy.51
  164.9 4.3 fusion.6
  169.2 7.2 %multiply_convert_fusion = (bf16[8,256,512]{1,2,0:T(8,128)(2,1)S(1)}, f32[8,256]{1,0:T(8,128)S(1)}) fusion(f32[8,256,512]{1,2,0:T(8,128)} %log_subtract_fusion.1, f32[256]{0:T(256)S(1)} %get-tuple-element.15, f32[8,256,512]{1,2,0:T(8,128)} %fusion.6), kind=kOutput, calls=%fused_computation.8 | output fusion | flops 7340543 | bytes 10494976 | tf_op jit(solution)/shard_map/reduce_sum | solution.py:25
  176.4 1.3 copy-done.1
  177.8 0.8 convolution_bitcast_fusion
  178.6 1.3 copy-done.2
  179.9 0.9 slice.15
  180.7 2.0 copy.42
  182.8 1.5 collective-permute-start.2
  184.2 3.3 fusion.23
  187.5 1.6 copy.43
  189.1 8.7 %collective-permute-done.2 = bf16[256,1024]{1,0:T(8,128)(2,1)} collective-permute-done((bf16[256,1024]{1,0:T(8,128)(2,1)}, bf16[256,1024]{1,0:T(8,128)(2,1)}, u32[]{:S(2)}, u32[]{:S(2)}) %collective-permute-start.2) | collective-permute-done | bytes 524320 | tf_op jit(solution)/shard_map/ppermute | solution.py:18
  197.8 6.7 %convert_bitcast_fusion = bf16[4096,1024]{0,1:T(8,128)(2,1)} fusion(bf16[1,256,4096]{2,1,0:T(8,128)(2,1)S(1)} %copy-done, f32[256,1024]{1,0:T(8,128)S(1)} %copy.43, bf16[256,1024]{1,0:T(8,128)(2,1)} %collective-permute-done.2), kind=kOutput, calls=%fused_computation.4 | convolution fusion | flops 2152464384 | bytes 12058624 | tf_op jit(solution)/shard_map/tr,tc->rc/dot_general | solution.py:102
  204.6 110.2 %reduce-scatter.5.cloned.1.call-done = bf16[256,1024]{0,1:T(8,128)(2,1)} async-done(((bf16[4096,1024]{0,1:T(8,128)(2,1)}), bf16[256,1024]{0,1:T(8,128)(2,1)}) %reduce-scatter.5.cloned.1.call-update) | async-done | bytes 524304 | tf_op jit(solution)/shard_map/reduce_scatter | solution.py:101
  314.8 0.6 multiply_reduce_fusion.1
  316.1 187.3 %psum.14 = f32[1]{0:T(128)} all-reduce(f32[1]{0:T(128)} %bitcast.8), channel_id=1, replica_groups=mesh['dp'=4,'ctx'=16,'tp'=4] {'ctx','tp'}, use_global_device_ids=true, to_apply=%region_7.8 | all-reduce | flops 1 | bytes 8 | tf_op jit(solution)/shard_map/psum | solution.py:110
  503.4 2.2 multiply_bitcast_fusion
  505.5 2.2 copy.44
  (21 shorter events, 0.3 us)
Async XLA Ops:
  8.0 133.2 %copy-start = (bf16[1,256,4096]{2,1,0:T(8,128)(2,1)S(1)}, bf16[1,256,4096]{2,1,0:T(8,128)(2,1)}, u32[]{:S(2)}) copy-start(bf16[1,256,4096]{2,1,0:T(8,128)(2,1)} %param.6) | copy-start | bytes 6291460
  8.0 57.3 %reduce-scatter.3.cloned.1.call-start = ((), (), s32[]{:S(2)}) async-start(), calls=%async_computation.2 | async-start | bytes 5242880 | tf_op jit(solution)/shard_map/reduce_scatter | solution.py:68
  14.6 54.9 %copy-start.4 = (s32[1,4096]{1,0:T(1,128)S(1)}, s32[1,4096]{1,0:T(1,128)}, u32[]{:S(2)}) copy-start(s32[1,4096]{1,0:T(1,128)} %param.8) | copy-start | bytes 49156
  14.6 126.6 %all-gather.2.cloned.1.call-start = ((), (), s32[]{:S(2)}) async-start(), calls=%async_computation.3 | async-start | bytes 8912896 | tf_op jit(solution)/shard_map/all_gather | solution.py:75
  15.2 299.6 %reduce-scatter.5.cloned.1.call-start = ((), (), s32[]{:S(2)}) async-start(), calls=%async_computation.4 | async-start | bytes 8912896 | tf_op jit(solution)/shard_map/reduce_scatter | solution.py:101
  65.4 49.3 %collective-permute-start = (bf16[256,2048]{0,1:T(8,128)(2,1)}, bf16[256,2048]{0,1:T(8,128)(2,1)S(1)}, u32[]{:S(2)}, u32[]{:S(2)}) collective-permute-start(bf16[256,2048]{0,1:T(8,128)(2,1)} %reduce-scatter.3.cloned.1.call-done), channel_id=1, source_target_pairs={{0,4},{4,8},{8,12},{12,16},{16,20},{20,24},{24,28},{28,32},{32,36}... | collective-permute-start | bytes 3145736 | tf_op jit(solution)/shard_map/ppermute | solution.py:18
  146.9 15.5 %collective-permute-start.1 = (bf16[256,1024]{1,0:T(8,128)(2,1)S(1)}, bf16[256,1024]{1,0:T(8,128)(2,1)S(1)}, u32[]{:S(2)}, u32[]{:S(2)}) collective-permute-start(bf16[256,1024]{1,0:T(8,128)(2,1)S(1)} %fusion.24), channel_id=1, source_target_pairs={{0,4},{4,8},{8,12},{12,16},{16,20},{20,24},{24,28},{28,32},{32,36}... | collective-permute-start | bytes 1572872 | tf_op jit(solution)/shard_map/ppermute | solution.py:18
  169.2 8.6 %copy-start.3 = (bf16[256,1024]{0,1:T(8,128)(2,1)S(1)}, bf16[256,1024]{0,1:T(8,128)(2,1)}, u32[]{:S(2)}) copy-start(bf16[256,1024]{0,1:T(8,128)(2,1)} %copy.50) | copy-start | bytes 1572868
  176.4 1.4 copy-start.1
  178.6 1.3 copy-start.2
  182.8 15.1 %collective-permute-start.2 = (bf16[256,1024]{1,0:T(8,128)(2,1)}, bf16[256,1024]{1,0:T(8,128)(2,1)}, u32[]{:S(2)}, u32[]{:S(2)}) collective-permute-start(bf16[256,1024]{1,0:T(8,128)(2,1)} %copy.42), channel_id=1, source_target_pairs={{4,0},{8,4},{12,8},{16,12},{20,16},{24,20},{28,24},{32,28},{36,32}... | collective-permute-start | bytes 1572872 | tf_op jit(solution)/shard_map/ppermute | solution.py:18
  204.5 301.0 %all-reduce.3.cloned.1.call-start = ((), (), s32[]{:S(2)}) async-start(), calls=%async_computation.5 | async-start | bytes 1048576 | tf_op jit(solution)/shard_map/psum | solution.py:109
Sparse Core Ops, SparseCore 0:
  14.7 50.6 reduce-scatter.2
  314.9 54.1 all-reduce.2
Sparse Core Ops, SparseCore 1:
  16.9 124.3 all-gather.1
  204.6 110.1 reduce-scatter.4
where the time goes:
time: 516 us; the launch traced here: 515 us
  waiting for transfers between devices  238 us (46%)
  blocking collectives  187 us (36%)
  matrix products  25.9 us (5%)
  other arithmetic  20.2 us (4%)
  local copies, waits for them, and re-layouts  18.4 us (4%)
  between operations  16.9 us (3%)
  starting transfers between devices  8.2 us (2%)
    psum x1, blocking collectives, per_device(): doc_loss = lax.psum(loss_part, ('ctx', 'tp'))  187 us
    reduce_scatter x1, waiting for transfers between devices, per_device(): lax.psum_scatter(jnp.einsum('tr,tc->rc', columns, hidden_grad, preferred_...  110 us
    ppermute x3, waiting for transfers between devices, shifted_2(): lax.ppermute(value, axis, [(source, source + steps) for source in range(l...  53.5 us
    reduce_scatter x1, waiting for transfers between devices, per_device(): lax.psum_scatter(partial_sum.astype(jnp.bfloat16), 'tp', scatter_dimensio...  50.1 us
    all_gather x1, waiting for transfers between devices, per_device(): lax.all_gather(out_proj, 'ctx', axis=0, tiled=True)  23.7 us
    reduce_sum x2, other arithmetic, log_probs(): return shifted - jnp.log(jnp.sum(jnp.exp(shifted), axis=-1, keepdims=True))  13.4 us
    unnamed x12, local copies, waits for them, and re-layouts  11.4 us
  transfers between devices with their start and end apart: 7, of which 5 were waited for; matrix products, arithmetic and copies ran while one was open for 4% of the time, Pallas kernels for 0%

commit v1 on v0

v1 whole, which is shorter than its diff:
```python
import math

import jax
import jax.numpy as jnp
from jax import lax
from jax.experimental import pallas as pl
from jax.experimental.pallas import tpu as pltpu
from jax.sharding import PartitionSpec as P

DS = 4096
HEADS = 32
MESH = pl.DeviceIdType.MESH
F32 = jnp.float32
BF16 = jnp.bfloat16
NEG = -1e30
UNSCALE = HEADS * math.sqrt(DS // HEADS)
T_SCALE = 1.0 / math.sqrt(256)
S_SCALE = 1.0 / math.sqrt(128)
G_SCALE = S_SCALE / HEADS
N_SEM = 224


def dot_nn(a, b):
    return lax.dot_general(a, b, (((1,), (0,)), ((), ())), preferred_element_type=F32)


def dot_nt(a, b):
    return lax.dot_general(a, b, (((1,), (1,)), ((), ())), preferred_element_type=F32)


def turned(a):
    return jnp.transpose(a.astype(F32)).astype(BF16)


def kernel(
    tpart, xin, win, seg_ref, valid_ref,
    ht_out, gt_out, loss_out,
    xb, wb, acc,
    t_own, t_fp, t_fm, r1p, r1m, rdp, rdm, r2p, r2m, tt, tx,
    ss, so, sx, st, sxt,
    mo, mp, mn, zt, lt, zs, st_d, st_n, rs_d, rs_n,
    hacc, hsend, hrecv, ho,
    gb, p1p, p1m, pdp, pdm, p2p, p2m, qb, q1p, q1m, qdp, qdm, q2p, q2m, fin, fin_r, gf, gf_r,
    lx, ly, lz,
    send_sem, recv_sem, loc_sem,
):
    dp, ctx, x = lax.axis_index("dp"), lax.axis_index("ctx"), lax.axis_index("tp")
    core, zh, zl, y = dp % 2, dp // 2, ctx // 4, ctx % 4
    z = zh * 4 + zl
    other = 1 - core

    def dev(x_, y_, z_, c_):
        return ((z_ // 4) * 2 + c_, (z_ % 4) * 4 + y_, x_)

    def on_x(k):
        return dev((x + k) % 4, y, z, core)

    def on_y(k):
        return dev(x, (y + k) % 4, z, core)

    def on_z(k):
        return dev(x, y, (z + k) % 8, core)

    def on_zl(k):
        return dev(x, y, zh * 4 + (zl + k) % 4, core)

    mate = dev(x, y, z, other)
    nxt = dev(x, (y + 1) % 4, (z + (y + 1) // 4) % 8, core)
    prv = dev(x, (y + 3) % 4, (z + 7 + (y + 3) // 4) % 8, core)

    partners = [on_x(1), on_x(2), on_x(3), on_y(1), on_y(2), on_y(3), on_z(1), on_z(7), on_z(4)]
    partners += [on_zl(1), on_zl(2), on_zl(3), mate, nxt, prv]

    sems = [0]
    pending = []

    def remote(src, dst, where):
        k = sems[0]
        sems[0] += 1
        return pltpu.make_async_remote_copy(
            src_ref=src, dst_ref=dst, send_sem=send_sem.at[k], recv_sem=recv_sem.at[k],
            device_id=where, device_id_type=MESH,
        )

    def go(copy):
        copy.start()
        pending.append(copy)
        return copy

    locs = [0]

    def local(src, dst):
        k = locs[0]
        locs[0] += 1
        copy = pltpu.make_async_copy(src, dst, loc_sem.at[k])
        copy.start()
        return copy

    x_loc = local(xin, xb.at[core])
    col0 = pl.multiple_of(core * 512, 512)
    w_loc = local(win.at[:, pl.ds(col0, 512)], wb.at[ctx])

    def tcol(block, head):
        return tpart.at[:, pl.ds(pl.multiple_of(block * 2048 + head * 256, 256), 256)]

    fp_loc = [local(tcol((x + 1) % 4, i), t_fp.at[i]) for i in range(4)]
    fm_loc = [local(tcol((x + 3) % 4, 4 + i), t_fm.at[i]) for i in range(4)]
    own_loc = [local(tcol(x, i), t_own.at[i]) for i in range(8)]

    barrier = pltpu.get_barrier_semaphore()
    for where in partners:
        pl.semaphore_signal(barrier, inc=1, device_id=where, device_id_type=MESH)
    pl.semaphore_wait(barrier, len(partners))

    m_s1p = [remote(tcol((x + 2) % 4, i), r1p.at[i], on_x(1)) for i in range(4)]
    m_s1m = [remote(tcol((x + 2) % 4, 4 + i), r1m.at[i], on_x(3)) for i in range(4)]
    m_dp = [remote(tcol((x + 1) % 4, 4 + i), rdp.at[i], on_x(1)) for i in range(4)]
    m_dm = [remote(tcol((x + 3) % 4, i), rdm.at[i], on_x(3)) for i in range(4)]
    m_s2p = [remote(r1p.at[i], r2p.at[i], on_x(1)) for i in range(4)]
    m_s2m = [remote(r1m.at[i], r2m.at[i], on_x(3)) for i in range(4)]
    m_ta = [remote(tt.at[i], tx.at[0, i], nxt) for i in range(4)]
    m_tb = [remote(tt.at[4 + i], tx.at[1, i], prv) for i in range(4)]
    m_x = remote(xin, xb.at[core], mate)

    def block(dy, dz):
        return ((zl + dz) % 4) * 4 + (y + dy) % 4

    def gather_messages(kind):
        base = kind * 128

        def at(dp_, dq_):
            return block(dq_, dp_) if kind == 0 else block(dp_, dq_)

        def to(which, sign):
            on_z_axis = (kind == 0) == (which == "p")
            k = 1 if sign > 0 else -1
            return on_z(k % 8) if on_z_axis else on_y(k % 4)

        def piece(dp_, dq_, part):
            start, size = {"all": (0, 128), "lo": (0, 64), "hi": (64, 64)}[part]
            b = at(dp_, dq_)
            return wb.at[b, pl.ds(base + start, size)]

        def message(dp_, dq_, part, which, sign):
            ref = piece(dp_, dq_, part)
            return remote(ref, ref, to(which, sign))

        own = win.at[pl.ds(base, 128), pl.ds(col0, 512)]

        def first(which, sign):
            return remote(own, piece(0, 0, "all"), to(which, sign))

        return [
            first("p", 1), first("p", -1), first("q", 1), first("q", -1),
            message(-1, 0, "lo", "p", 1), message(1, 0, "hi", "p", -1),
            message(-1, 0, "all", "q", 1), message(-1, 0, "all", "q", -1),
            message(1, 0, "all", "q", 1), message(1, 0, "all", "q", -1),
            message(0, -1, "lo", "q", 1), message(0, 1, "hi", "q", -1),
            message(2, 0, "all", "q", 1), message(2, 0, "all", "q", -1),
            message(-1, -1, "lo", "q", 1), message(-1, 1, "hi", "q", -1),
            message(1, -1, "lo", "q", 1), message(1, 1, "hi", "q", -1),
            message(2, -1, "lo", "q", 1), message(2, 1, "hi", "q", -1),
        ]

    ag = [gather_messages(0), gather_messages(1)]

    def ag_start(*ids):
        for k in ids:
            for kind in (0, 1):
                go(ag[kind][k])

    def ag_wait(*ids):
        for k in ids:
            for kind in (0, 1):
                ag[kind][k].wait_recv()

    go(m_s1p[0]); go(m_s1m[0])
    ag_start(0, 1)
    go(m_s1p[1]); go(m_s1m[1]); go(m_dp[0]); go(m_dm[0])
    ag_start(2, 3)
    go(m_x)

    window = ctx
    valid = valid_ref[0]

    def seg_row(w):
        return seg_ref[:, pl.ds(pl.multiple_of(w * 256, 256), 256)].astype(F32)

    row_own = seg_row(window)
    row_next = seg_row((window + 1) % 16)
    col_own = jnp.transpose(jnp.broadcast_to(row_own, (256, 256)))
    col_prev = jnp.transpose(jnp.broadcast_to(seg_row((window + 15) % 16), (256, 256)))
    key_iota = lax.broadcasted_iota(jnp.int32, (256, 256), 0)
    query_iota = lax.broadcasted_iota(jnp.int32, (256, 256), 1)
    key_own = key_iota + window * 256
    key_prev = key_own - 256
    query_next = query_iota + (window + 1) * 256
    mo[...] = jnp.where((col_own == row_own) & (key_own < valid), 0.0, NEG)
    mp[...] = jnp.where((col_prev == row_own) & (key_prev >= 0) & (key_prev < valid), 0.0, NEG)
    mn[...] = jnp.where((col_own == row_next) & (key_own < valid) & (query_next < 4096), 0.0, NEG)
    lane = lax.broadcasted_iota(jnp.int32, (1, 256), 1)
    live_own = jnp.where(lane + window * 256 < valid, 1.0, 0.0).astype(F32)
    live_next = jnp.where(
        (lane + (window + 1) * 256 < valid) & (lane + (window + 1) * 256 < 4096), 1.0, 0.0
    ).astype(F32)

    acc[...] = jnp.zeros_like(acc)

    def feed(dy, dz):
        b = block(dy, dz)
        xs = xb[:, :, pl.ds(pl.multiple_of(b * 256, 256), 256)].reshape(512, 256)
        acc[...] += dot_nn(xs, wb[b])

    def relay(i):
        m_s1p[i].wait_recv()
        fp_loc[i].wait()
        r1p[i] = (r1p[i].astype(F32) + t_fp[i].astype(F32)).astype(BF16)
        go(m_s2p[i])
        m_s1m[i].wait_recv()
        fm_loc[i].wait()
        r1m[i] = (r1m[i].astype(F32) + t_fm[i].astype(F32)).astype(BF16)
        go(m_s2m[i])

    def settle(i):
        m_s2p[i].wait_recv()
        m_dm[i].wait_recv()
        own_loc[i].wait()
        tt[i] = (t_own[i].astype(F32) + r2p[i].astype(F32) + rdm[i].astype(F32)).astype(BF16)
        go(m_ta[i])
        m_s2m[i].wait_recv()
        m_dp[i].wait_recv()
        own_loc[4 + i].wait()
        tt[4 + i] = (
            t_own[4 + i].astype(F32) + r2m[i].astype(F32) + rdp[i].astype(F32)
        ).astype(BF16)
        go(m_tb[i])

    ag_wait(0, 1)
    ag_start(4, 5, 6, 7, 8, 9)
    relay(0)
    go(m_s1p[2]); go(m_s1m[2]); go(m_dp[1]); go(m_dm[1])
    ag_wait(2, 3)
    ag_start(10, 11)
    relay(1)
    go(m_s1p[3]); go(m_s1m[3]); go(m_dp[2]); go(m_dm[2])
    x_loc.wait()
    w_loc.wait()
    m_x.wait_recv()
    feed(0, 0)
    feed(1, 0)
    feed(-1, 0)
    feed(0, 1)
    feed(0, -1)
    ag_wait(4, 5)
    ag_start(12, 13)
    settle(0)
    ag_wait(6, 7, 8, 9)
    ag_start(14, 15, 16, 17)
    relay(2)
    go(m_dp[3]); go(m_dm[3])
    feed(1, 1)
    feed(-1, 1)
    feed(1, -1)
    feed(-1, -1)
    ag_wait(12, 13)
    ag_start(18, 19)
    settle(1)
    relay(3)
    ag_wait(10, 11)
    feed(2, 0)
    feed(0, 2)
    ag_wait(14, 15, 16, 17)
    feed(2, 1)
    feed(2, -1)
    feed(1, 2)
    feed(-1, 2)
    ag_wait(18, 19)
    feed(2, 2)

    m_so = remote(so, ss.at[pl.ds(core * 4, 4)], mate)

    def half_to(f):
        up = 1 - f
        y_ = (y + 1 + 2 * f) % 4
        z_ = (z + up * ((y + 1) // 4) + f * (7 + (y + 3) // 4)) % 8
        return dev(x, y_, z_, core)

    k_half = sems[0]
    sems[0] += 2

    def half_copy(f):
        return pltpu.make_async_remote_copy(
            src_ref=ss.at[pl.ds(f * 4, 4)], dst_ref=sx.at[f], send_sem=send_sem.at[k_half + f],
            recv_sem=recv_sem.at[k_half + f], device_id=half_to(f), device_id_type=MESH,
        )

    acc_own = acc[pl.ds(pl.multiple_of(core * 256, 256), 256), :].astype(BF16)
    acc_oth = acc[pl.ds(pl.multiple_of(other * 256, 256), 256), :].astype(BF16)
    for j in range(4):
        so[j] = acc_oth[:, j * 128:(j + 1) * 128]
    go(m_so)
    for j in range(4):
        ss[core * 4 + j] = acc_own[:, j * 128:(j + 1) * 128]
    go(half_copy(core))
    m_so.wait_recv()
    go(half_copy(other))

    def teacher_a(i):
        m_ta[i].wait_recv()
        q = tt[i]
        own = dot_nt(q, q) * T_SCALE + mo[...]
        off = dot_nt(tx[0, i], q) * T_SCALE + mp[...]
        top = jnp.maximum(jnp.max(own, 0, keepdims=True), jnp.max(off, 0, keepdims=True))
        own = own - top
        off = off - top
        zt[i, 0] = own
        zt[i, 1] = off
        total = jnp.sum(jnp.exp(own), 0, keepdims=True) + jnp.sum(jnp.exp(off), 0, keepdims=True)
        lt[i:i + 1] = jnp.log(total)

    def b_stats(own, off, row):
        top = jnp.max(own, 0, keepdims=True)
        own = own - top
        st_d[row:row + 1] = top
        st_d[row + 4:row + 5] = jnp.sum(jnp.exp(own), 0, keepdims=True)
        top = jnp.max(off, 0, keepdims=True)
        off = off - top
        st_n[row:row + 1] = top
        st_n[row + 4:row + 5] = jnp.sum(jnp.exp(off), 0, keepdims=True)
        return own, off

    def teacher_b(i):
        m_tb[i].wait_recv()
        k = tt[4 + i]
        own = dot_nt(k, k) * T_SCALE + mo[...]
        off = dot_nt(k, tx[1, i]) * T_SCALE + mn[...]
        zt[4 + i, 0], zt[4 + i, 1] = b_stats(own, off, i)

    settle(2)
    teacher_a(0)
    teacher_b(0)
    teacher_a(1)
    teacher_b(1)
    settle(3)
    for j in range(8):
        st[j] = turned(ss[j])
    teacher_a(2)
    teacher_b(2)
    for f in range(2):
        half_copy(f).wait_recv()
        for j in range(4):
            sxt[f, j] = turned(sx[f, j])

    for i in range(4):
        k = ss[4 + i]
        own = dot_nt(k, k) * S_SCALE + mo[...]
        off = dot_nt(k, sx[1, i]) * S_SCALE + mn[...]
        zs[i, 0], zs[i, 1] = b_stats(own, off, 8 + i)
    teacher_b(3)
    m_sd = go(remote(st_d, rs_d, prv))
    m_sn = go(remote(st_n, rs_n, nxt))
    teacher_a(3)

    gain_own = live_own * G_SCALE
    gain_next = live_next * G_SCALE

    def grads(t_log, s_log, live, gain):
        t_prob = jnp.exp(t_log)
        s_prob = jnp.exp(s_log)
        loss = jnp.sum(t_prob * (t_log - s_log), 0, keepdims=True) * live
        return loss, ((s_prob - t_prob) * gain).astype(BF16)

    m_h = [remote(hsend.at[i], hrecv.at[i], prv if i < 4 else nxt) for i in range(8)]
    losses = []

    def relate_a(i):
        q = ss[i]
        own = dot_nt(q, q) * S_SCALE + mo[...]
        off = dot_nt(sx[0, i], q) * S_SCALE + mp[...]
        top = jnp.maximum(jnp.max(own, 0, keepdims=True), jnp.max(off, 0, keepdims=True))
        own = own - top
        off = off - top
        total = jnp.sum(jnp.exp(own), 0, keepdims=True) + jnp.sum(jnp.exp(off), 0, keepdims=True)
        s_sum = jnp.log(total)
        t_sum = lt[i:i + 1]
        loss_o, g_own = grads(zt[i, 0] - t_sum, own - s_sum, live_own, gain_own)
        loss_p, g_off = grads(zt[i, 1] - t_sum, off - s_sum, live_own, gain_own)
        losses.append(loss_o + loss_p)
        turned_q = st[i]
        hsend[i] = dot_nt(turned_q, g_off).astype(BF16)
        go(m_h[i])
        hacc[i] = dot_nn(sxt[0, i], g_off) + dot_nn(turned_q, g_own) + dot_nt(turned_q, g_own)

    def shifts(m_here, l_here, m_there, l_there):
        top = jnp.maximum(m_here, m_there)
        total = l_here * jnp.exp(m_here - top) + l_there * jnp.exp(m_there - top)
        return (m_here - top) - jnp.log(total)

    def relate_b(i):
        def row(ref, r):
            return ref[r:r + 1]

        t_own = shifts(row(st_d, i), row(st_d, 4 + i), row(rs_n, i), row(rs_n, 4 + i))
        s_own = shifts(row(st_d, 8 + i), row(st_d, 12 + i), row(rs_n, 8 + i), row(rs_n, 12 + i))
        t_off = shifts(row(st_n, i), row(st_n, 4 + i), row(rs_d, i), row(rs_d, 4 + i))
        s_off = shifts(row(st_n, 8 + i), row(st_n, 12 + i), row(rs_d, 8 + i), row(rs_d, 12 + i))
        loss_o, g_own = grads(zt[4 + i, 0] + t_own, zs[i, 0] + s_own, live_own, gain_own)
        loss_n, g_off = grads(zt[4 + i, 1] + t_off, zs[i, 1] + s_off, live_next, gain_next)
        losses.append(loss_o + loss_n)
        turned_k = st[4 + i]
        hsend[4 + i] = dot_nn(turned_k, g_off).astype(BF16)
        go(m_h[4 + i])
        hacc[4 + i] = dot_nn(turned_k, g_own) + dot_nt(turned_k, g_own) + dot_nt(sxt[1, i], g_off)

    def finish(i):
        m_h[i].wait_recv()
        ht_out[pl.ds(i * 128, 128), :] = (hacc[i] + hrecv[i].astype(F32)).astype(BF16)

    m_ho = [
        remote(ht_out.at[pl.ds(pl.multiple_of(other * 512 + j * 128, 128), 128)], ho.at[j], mate)
        for j in range(4)
    ]

    first_y = [True, False, True, True]

    def chunk(j):
        m_ho[j].wait_recv()
        mine = ht_out[pl.ds(pl.multiple_of(core * 512 + j * 128, 128), 128), :]
        theirs = ho[j]
        for k in range(4):
            part = dot_nn(mine, xb[core, :, k * 1024:(k + 1) * 1024])
            part = part + dot_nn(theirs, xb[other, :, k * 1024:(k + 1) * 1024])
            part = part.astype(BF16)
            for m in range(4):
                piece = part[:, m * 256:(m + 1) * 256]
                if first_y[j]:
                    gb[j, m, k] = piece
                else:
                    gb[j, k, m] = piece

    class Ring:
        def __init__(self, j, along_y, unit, bufs, halves):
            self.me = y if along_y else zl
            up = on_y(1) if along_y else on_z(1)
            down = on_y(3) if along_y else on_z(7)
            self.unit, self.halves = unit, halves
            self.b1p, self.b1m, self.bdp, self.bdm, self.b2p, self.b2m = [b.at[j] for b in bufs]
            lo, hi = halves
            self.s1p = remote(self.at(2, lo), self.b1p, up)
            self.s1m = remote(self.at(2, hi), self.b1m, down)
            self.dp = remote(self.at(1, hi), self.bdp, up)
            self.dm = remote(self.at(3, lo), self.bdm, down)
            self.s2p = remote(self.b1p, self.b2p, up)
            self.s2m = remote(self.b1m, self.b2m, down)

        def at(self, k, half):
            return self.unit.at[(self.me + k) % 4].at[half]

        def open(self):
            go(self.s1p); go(self.s1m); go(self.dp); go(self.dm)

        def middle(self):
            lo, hi = self.halves
            self.s1p.wait_recv()
            self.b1p[...] = (
                self.b1p[...].astype(F32) + self.at(1, lo)[...].astype(F32)
            ).astype(BF16)
            go(self.s2p)
            self.s1m.wait_recv()
            self.b1m[...] = (
                self.b1m[...].astype(F32) + self.at(3, hi)[...].astype(F32)
            ).astype(BF16)
            go(self.s2m)

        def close(self, dst):
            lo, hi = self.halves
            self.s2p.wait_recv()
            self.dm.wait_recv()
            dst.at[lo][...] = (
                self.at(0, lo)[...].astype(F32) + self.b2p[...].astype(F32)
                + self.bdm[...].astype(F32)
            ).astype(BF16)
            self.s2m.wait_recv()
            self.dp.wait_recv()
            dst.at[hi][...] = (
                self.at(0, hi)[...].astype(F32) + self.b2m[...].astype(F32)
                + self.bdp[...].astype(F32)
            ).astype(BF16)

    p_ring = [
        Ring(j, first_y[j], gb.at[j], (p1p, p1m, pdp, pdm, p2p, p2m), (pl.ds(0, 2), pl.ds(2, 2)))
        for j in range(4)
    ]
    q_ring = [
        Ring(j, not first_y[j], qb.at[j], (q1p, q1m, qdp, qdm, q2p, q2m),
             (pl.ds(0, 64), pl.ds(64, 64)))
        for j in range(4)
    ]
    m_fin = [remote(fin.at[j], fin_r.at[j], on_z(4)) for j in range(4)]
    m_gf = [remote(gf.at[j], gf_r.at[j], mate) for j in range(4)]

    def to_q(j):
        p_ring[j].close(qb.at[j])
        q_ring[j].open()

    def to_pair(j):
        q_ring[j].close(fin.at[j])
        go(m_fin[j])

    def total(j):
        m_fin[j].wait_recv()
        gf[j] = fin[j].astype(F32) + fin_r[j].astype(F32)
        go(m_gf[j])

    def emit(j):
        m_gf[j].wait_recv()
        gt_out[pl.ds(pl.multiple_of(core * 512 + j * 128, 128), 128), :] = gf[j]
        gt_out[pl.ds(pl.multiple_of(other * 512 + j * 128, 128), 128), :] = gf_r[j]

    def spread(buf, me, where):
        return [go(remote(buf.at[me], buf.at[me], where(k))) for k in (1, 2, 3)]

    def gathered(copies, buf):
        for copy in copies:
            copy.wait_recv()
        return buf[0] + buf[1] + buf[2] + buf[3]

    for i in range(4):
        relate_a(i)
    m_sd.wait_recv()
    m_sn.wait_recv()
    relate_b(0)
    finish(0); finish(4); go(m_ho[0])
    relate_b(1)
    finish(1); finish(5); go(m_ho[1])
    chunk(0)
    p_ring[0].open()
    relate_b(2)
    finish(2); finish(6); go(m_ho[2])
    chunk(1)
    p_ring[1].open()
    relate_b(3)
    finish(3); finish(7); go(m_ho[3])
    p_ring[0].middle()
    chunk(2)
    p_ring[2].open()
    loss = losses[0]
    for part in losses[1:]:
        loss = loss + part
    loss = jnp.sum(loss, keepdims=True) * (1.0 / HEADS)
    lx[x] = jnp.broadcast_to(loss, (8, 128))
    c_x = spread(lx, x, on_x)
    p_ring[1].middle()
    chunk(3)
    p_ring[3].open()
    to_q(0)
    p_ring[2].middle()
    ly[y] = gathered(c_x, lx)
    c_y = spread(ly, y, on_y)
    to_q(1)
    q_ring[0].middle()
    p_ring[3].middle()
    to_q(2)
    q_ring[1].middle()
    lz[zl] = gathered(c_y, ly)
    c_z = spread(lz, zl, on_zl)
    to_pair(0)
    to_q(3)
    q_ring[2].middle()
    to_pair(1)
    total(0)
    q_ring[3].middle()
    to_pair(2)
    total(1)
    emit(0)
    to_pair(3)
    loss_out[...] = gathered(c_z, lz)
    total(2)
    emit(1)
    total(3)
    emit(2)
    emit(3)
    for copy in pending:
        copy.wait_send()


def per_device(teacher_part, student_in, out_proj, segment_ids, valid_count):
    anywhere = pl.BlockSpec(memory_space=pl.ANY)
    vmem = pl.BlockSpec(memory_space=pltpu.VMEM)

    def b(*shape):
        return pltpu.VMEM(shape, BF16)

    def f(*shape):
        return pltpu.VMEM(shape, F32)

    scratch = [b(2, 256, 4096), b(16, 256, 512), f(512, 512)]
    scratch += [b(8, 256, 256)] + [b(4, 256, 256)] * 8 + [b(8, 256, 256), b(2, 4, 256, 256)]
    scratch += [b(8, 256, 128), b(4, 256, 128), b(2, 4, 256, 128), b(8, 128, 256), b(2, 4, 128, 256)]
    scratch += [f(256, 256)] * 3 + [f(8, 2, 256, 256), f(8, 256), f(4, 2, 256, 256)]
    scratch += [f(16, 256)] * 4
    scratch += [f(8, 128, 256), b(8, 128, 256), b(8, 128, 256), b(4, 128, 256)]
    scratch += [b(4, 4, 4, 128, 256)] + [b(4, 2, 128, 256)] * 6
    scratch += [b(4, 4, 128, 256)] + [b(4, 64, 256)] * 6
    scratch += [b(4, 128, 256)] * 2 + [f(4, 128, 256)] * 2
    scratch += [f(4, 8, 128)] * 3
    scratch += [
        pltpu.SemaphoreType.DMA((N_SEM,)), pltpu.SemaphoreType.DMA((N_SEM,)),
        pltpu.SemaphoreType.DMA((24,)),
    ]
    ht, gt, loss = pl.pallas_call(
        kernel,
        out_shape=(
            jax.ShapeDtypeStruct((1024, 256), BF16),
            jax.ShapeDtypeStruct((1024, 256), F32),
            jax.ShapeDtypeStruct((8, 128), F32),
        ),
        in_specs=[anywhere, anywhere, anywhere, vmem, pl.BlockSpec(memory_space=pltpu.SMEM)],
        out_specs=(vmem, vmem, vmem),
        scratch_shapes=scratch,
        name="relation_step",
        compiler_params=pltpu.CompilerParams(
            collective_id=0, has_side_effects=True, vmem_limit_bytes=60 * 2**20
        ),
    )(teacher_part[0, 0], student_in[0], out_proj, segment_ids, valid_count)
    state_grad = (ht.T.astype(F32) * UNSCALE)[None]
    return (loss[0, :1], gt.T, state_grad)


def solution(mesh):
    return jax.shard_map(
        per_device,
        mesh=mesh,
        in_specs=(
            P("dp", "tp", "ctx", None),
            P("dp", "ctx", None),
            P("ctx", "tp"),
            P("dp", None),
            P("dp"),
        ),
        out_specs=(P("dp"), P("ctx", "tp"), P("dp", "ctx", "tp")),
        check_vma=False,
    )
```

time: 516 us -> 138 us (0.27)
  the two profiles are of different devices: /device:TPU:0 before, /device:TPU:9 now
where the time goes in v1:
time: 138 us
  Pallas kernels  130 us (94%)
  local copies, waits for them, and re-layouts  5.03 us (4%)
    pallas_call x1, Pallas kernels, per_device(): pl.pallas_call(kernel, out_shape=(jax.ShapeDtypeStruct((1024, 256), BF16)...  130 us
    unnamed x2, local copies, waits for them, and re-layouts  3.84 us

profile of v1, /device:TPU:9, one launch (start us, length us, event | category | flops | bytes accessed | tf_op | source)
XLA Modules:
  0.0 137.9 jit_solution(8354172678839253043)
XLA Ops:
  1.3 130.5 %relation_step.1 = (bf16[1024,256]{1,0:T(8,128)(2,1)}, f32[1024,256]{1,0:T(8,128)}, f32[8,128]{1,0:T(8,128)}) custom-call(bf16[256,8192]{1,0:T(8,128)(2,1)} %bitcast.8, bf16[256,4096]{1,0:T(8,128)(2,1)} %bitcast.9, bf16[256,1024]{1,0:T(8,128)(2,1)} %win.1, s32[1,4096]{1,0:T(1,128)} %seg_ref.1, s32[1]{0:T(128)S(6)} %copy.10.valid_ref), custom_call_target="tpu_custom_call" | custom-call | tf_op jit(solution)/shard_map/relation_step/pallas_call | solution.py:611
  131.7 1.2 slice.3
  132.9 2.5 %copy.8 = f32[256,1024]{1,0:T(8,128)} copy(f32[256,1024]{0,1:T(8,128)} %bitcast.10) | data formatting | bytes 2097152
  135.5 1.1 multiply_bitcast_fusion
  136.6 1.3 copy.9

commit v2 on v1

--- a/solution.py
+++ b/solution.py
@@ -34,13 +34,13 @@
 
 def kernel(
     tpart, xin, win, seg_ref, valid_ref,
-    ht_out, gt_out, loss_out,
+    h_out, gt_out, loss_out,
     xb, wb, acc,
     t_own, t_fp, t_fm, r1p, r1m, rdp, rdm, r2p, r2m, tt, tx,
     ss, so, sx, st, sxt,
     mo, mp, mn, zt, lt, zs, st_d, st_n, rs_d, rs_n,
-    hacc, hsend, hrecv, ho,
-    gb, p1p, p1m, pdp, pdm, p2p, p2m, qb, q1p, q1m, qdp, qdm, q2p, q2m, fin, fin_r, gf, gf_r,
+    hacc, hsend, hrecv, ht, ho,
+    gb, p1p, p1m, pdp, pdm, p2p, p2m, qb, q1p, q1m, qdp, qdm, q2p, q2m, fin, fin_m, fin_r, gf, gf_r,
     lx, ly, lz,
     send_sem, recv_sem, loc_sem,
 ):
@@ -68,8 +68,7 @@
     nxt = dev(x, (y + 1) % 4, (z + (y + 1) // 4) % 8, core)
     prv = dev(x, (y + 3) % 4, (z + 7 + (y + 3) // 4) % 8, core)
 
-    partners = [on_x(1), on_x(2), on_x(3), on_y(1), on_y(2), on_y(3), on_z(1), on_z(7), on_z(4)]
-    partners += [on_zl(1), on_zl(2), on_zl(3), mate, nxt, prv]
+    partners = [on_x(1), on_x(3), on_y(1), on_y(3), on_z(1), on_z(7), mate]
 
     sems = [0]
     pending = []
@@ -241,21 +240,21 @@
     go(m_s1p[2]); go(m_s1m[2]); go(m_dp[1]); go(m_dm[1])
     ag_wait(2, 3)
     ag_start(10, 11)
-    relay(1)
-    go(m_s1p[3]); go(m_s1m[3]); go(m_dp[2]); go(m_dm[2])
     x_loc.wait()
     w_loc.wait()
     m_x.wait_recv()
     feed(0, 0)
+    relay(1)
+    go(m_s1p[3]); go(m_s1m[3]); go(m_dp[2]); go(m_dm[2])
+    ag_wait(4, 5)
+    ag_start(12, 13)
     feed(1, 0)
     feed(-1, 0)
     feed(0, 1)
     feed(0, -1)
-    ag_wait(4, 5)
-    ag_start(12, 13)
-    settle(0)
     ag_wait(6, 7, 8, 9)
     ag_start(14, 15, 16, 17)
+    settle(0)
     relay(2)
     go(m_dp[3]); go(m_dm[3])
     feed(1, 1)
@@ -264,16 +263,16 @@
     feed(-1, -1)
     ag_wait(12, 13)
     ag_start(18, 19)
-    settle(1)
-    relay(3)
     ag_wait(10, 11)
     feed(2, 0)
     feed(0, 2)
+    settle(1)
     ag_wait(14, 15, 16, 17)
     feed(2, 1)
     feed(2, -1)
     feed(1, 2)
     feed(-1, 2)
+    relay(3)
     ag_wait(18, 19)
     feed(2, 2)
 
@@ -286,12 +285,13 @@
         return dev(x, y_, z_, core)
 
     k_half = sems[0]
-    sems[0] += 2
-
-    def half_copy(f):
+    sems[0] += 8
+
+    def half_copy(f, j):
+        k = k_half + f * 4 + j
         return pltpu.make_async_remote_copy(
-            src_ref=ss.at[pl.ds(f * 4, 4)], dst_ref=sx.at[f], send_sem=send_sem.at[k_half + f],
-            recv_sem=recv_sem.at[k_half + f], device_id=half_to(f), device_id_type=MESH,
+            src_ref=ss.at[f * 4 + j], dst_ref=sx.at[f, j], send_sem=send_sem.at[k],
+            recv_sem=recv_sem.at[k], device_id=half_to(f), device_id_type=MESH,
         )
 
     acc_own = acc[pl.ds(pl.multiple_of(core * 256, 256), 256), :].astype(BF16)
@@ -301,9 +301,12 @@
     go(m_so)
     for j in range(4):
         ss[core * 4 + j] = acc_own[:, j * 128:(j + 1) * 128]
-    go(half_copy(core))
+        go(half_copy(core, j))
+    for j in range(4):
+        st[core * 4 + j] = turned(acc_own[:, j * 128:(j + 1) * 128])
     m_so.wait_recv()
-    go(half_copy(other))
+    for j in range(4):
+        go(half_copy(other, j))
 
     def teacher_a(i):
         m_ta[i].wait_recv()
@@ -318,15 +321,15 @@
         total = jnp.sum(jnp.exp(own), 0, keepdims=True) + jnp.sum(jnp.exp(off), 0, keepdims=True)
         lt[i:i + 1] = jnp.log(total)
 
-    def b_stats(own, off, row):
+    def b_stats(own, off, i, row):
         top = jnp.max(own, 0, keepdims=True)
         own = own - top
-        st_d[row:row + 1] = top
-        st_d[row + 4:row + 5] = jnp.sum(jnp.exp(own), 0, keepdims=True)
+        st_d[i, row:row + 1] = top
+        st_d[i, row + 1:row + 2] = jnp.sum(jnp.exp(own), 0, keepdims=True)
         top = jnp.max(off, 0, keepdims=True)
         off = off - top
-        st_n[row:row + 1] = top
-        st_n[row + 4:row + 5] = jnp.sum(jnp.exp(off), 0, keepdims=True)
+        st_n[i, row:row + 1] = top
+        st_n[i, row + 1:row + 2] = jnp.sum(jnp.exp(off), 0, keepdims=True)
         return own, off
 
     def teacher_b(i):
@@ -334,32 +337,23 @@
         k = tt[4 + i]
         own = dot_nt(k, k) * T_SCALE + mo[...]
         off = dot_nt(k, tx[1, i]) * T_SCALE + mn[...]
-        zt[4 + i, 0], zt[4 + i, 1] = b_stats(own, off, i)
-
-    settle(2)
-    teacher_a(0)
-    teacher_b(0)
-    teacher_a(1)
-    teacher_b(1)
-    settle(3)
-    for j in range(8):
-        st[j] = turned(ss[j])
-    teacher_a(2)
-    teacher_b(2)
-    for f in range(2):
-        half_copy(f).wait_recv()
-        for j in range(4):
-            sxt[f, j] = turned(sx[f, j])
-
-    for i in range(4):
+        zt[4 + i, 0], zt[4 + i, 1] = b_stats(own, off, i, 0)
+
+    m_sd = [remote(st_d.at[i], rs_d.at[i], prv) for i in range(4)]
+    m_sn = [remote(st_n.at[i], rs_n.at[i], nxt) for i in range(4)]
+
+    def student_b(i):
+        half_copy(1, i).wait_recv()
         k = ss[4 + i]
         own = dot_nt(k, k) * S_SCALE + mo[...]
         off = dot_nt(k, sx[1, i]) * S_SCALE + mn[...]
-        zs[i, 0], zs[i, 1] = b_stats(own, off, 8 + i)
-    teacher_b(3)
-    m_sd = go(remote(st_d, rs_d, prv))
-    m_sn = go(remote(st_n, rs_n, nxt))
-    teacher_a(3)
+        zs[i, 0], zs[i, 1] = b_stats(own, off, i, 2)
+        go(m_sd[i])
+        go(m_sn[i])
+        sxt[1, i] = turned(sx[1, i])
+
+    def turn_own(j):
+        st[other * 4 + j] = turned(ss[other * 4 + j])
 
     gain_own = live_own * G_SCALE
     gain_next = live_next * G_SCALE
@@ -374,6 +368,8 @@
     losses = []
 
     def relate_a(i):
+        half_copy(0, i).wait_recv()
+        sxt[0, i] = turned(sx[0, i])
         q = ss[i]
         own = dot_nt(q, q) * S_SCALE + mo[...]
         off = dot_nt(sx[0, i], q) * S_SCALE + mp[...]
@@ -397,13 +393,16 @@
         return (m_here - top) - jnp.log(total)
 
     def relate_b(i):
+        m_sd[i].wait_recv()
+        m_sn[i].wait_recv()
+
         def row(ref, r):
-            return ref[r:r + 1]
-
-        t_own = shifts(row(st_d, i), row(st_d, 4 + i), row(rs_n, i), row(rs_n, 4 + i))
-        s_own = shifts(row(st_d, 8 + i), row(st_d, 12 + i), row(rs_n, 8 + i), row(rs_n, 12 + i))
-        t_off = shifts(row(st_n, i), row(st_n, 4 + i), row(rs_d, i), row(rs_d, 4 + i))
-        s_off = shifts(row(st_n, 8 + i), row(st_n, 12 + i), row(rs_d, 8 + i), row(rs_d, 12 + i))
+            return ref[i, r:r + 1]
+
+        t_own = shifts(row(st_d, 0), row(st_d, 1), row(rs_n, 0), row(rs_n, 1))
+        s_own = shifts(row(st_d, 2), row(st_d, 3), row(rs_n, 2), row(rs_n, 3))
+        t_off = shifts(row(st_n, 0), row(st_n, 1), row(rs_d, 0), row(rs_d, 1))
+        s_off = shifts(row(st_n, 2), row(st_n, 3), row(rs_d, 2), row(rs_d, 3))
         loss_o, g_own = grads(zt[4 + i, 0] + t_own, zs[i, 0] + s_own, live_own, gain_own)
         loss_n, g_off = grads(zt[4 + i, 1] + t_off, zs[i, 1] + s_off, live_next, gain_next)
         losses.append(loss_o + loss_n)
@@ -412,20 +411,26 @@
         go(m_h[4 + i])
         hacc[4 + i] = dot_nn(turned_k, g_own) + dot_nt(turned_k, g_own) + dot_nt(sxt[1, i], g_off)
 
-    def finish(i):
+    def finish_one(i):
         m_h[i].wait_recv()
-        ht_out[pl.ds(i * 128, 128), :] = (hacc[i] + hrecv[i].astype(F32)).astype(BF16)
-
-    m_ho = [
-        remote(ht_out.at[pl.ds(pl.multiple_of(other * 512 + j * 128, 128), 128)], ho.at[j], mate)
-        for j in range(4)
-    ]
+        full = (hacc[i] + hrecv[i].astype(F32)).astype(BF16)
+        ht[i] = full
+        return full
+
+    m_ho = [remote(ht.at[other * 4 + j], ho.at[j], mate) for j in range(4)]
+
+    def finish(j):
+        low = finish_one(j)
+        high = finish_one(4 + j)
+        go(m_ho[j])
+        h_out[:, j * 128:(j + 1) * 128] = turned(low)
+        h_out[:, (4 + j) * 128:(5 + j) * 128] = turned(high)
 
     first_y = [True, False, True, True]
 
     def chunk(j):
         m_ho[j].wait_recv()
-        mine = ht_out[pl.ds(pl.multiple_of(core * 512 + j * 128, 128), 128), :]
+        mine = ht[core * 4 + j]
         theirs = ho[j]
         for k in range(4):
             part = dot_nn(mine, xb[core, :, k * 1024:(k + 1) * 1024])
@@ -496,7 +501,17 @@
              (pl.ds(0, 64), pl.ds(64, 64)))
         for j in range(4)
     ]
-    m_fin = [remote(fin.at[j], fin_r.at[j], on_z(4)) for j in range(4)]
+    low, high = pl.ds(0, 64), pl.ds(64, 64)
+    m_f1 = [
+        (remote(fin.at[j, low], fin_m.at[j, low], on_z(2)),
+         remote(fin.at[j, high], fin_m.at[j, high], on_z(6)))
+        for j in range(4)
+    ]
+    m_f2 = [
+        (remote(fin_m.at[j, low], fin_r.at[j, low], on_z(2)),
+         remote(fin_m.at[j, high], fin_r.at[j, high], on_z(6)))
+        for j in range(4)
+    ]
     m_gf = [remote(gf.at[j], gf_r.at[j], mate) for j in range(4)]
 
     def to_q(j):
@@ -505,17 +520,24 @@
 
     def to_pair(j):
         q_ring[j].close(fin.at[j])
-        go(m_fin[j])
+        for copy in m_f1[j]:
+            go(copy)
+
+    def pass_on(j):
+        for come, leave in zip(m_f1[j], m_f2[j]):
+            come.wait_recv()
+            go(leave)
 
     def total(j):
-        m_fin[j].wait_recv()
+        for copy in m_f2[j]:
+            copy.wait_recv()
         gf[j] = fin[j].astype(F32) + fin_r[j].astype(F32)
         go(m_gf[j])
+        gt_out[:, pl.ds(pl.multiple_of(core * 512 + j * 128, 128), 128)] = jnp.transpose(gf[j])
 
     def emit(j):
         m_gf[j].wait_recv()
-        gt_out[pl.ds(pl.multiple_of(core * 512 + j * 128, 128), 128), :] = gf[j]
-        gt_out[pl.ds(pl.multiple_of(other * 512 + j * 128, 128), 128), :] = gf_r[j]
+        gt_out[:, pl.ds(pl.multiple_of(other * 512 + j * 128, 128), 128)] = jnp.transpose(gf_r[j])
 
     def spread(buf, me, where):
         return [go(remote(buf.at[me], buf.at[me], where(k))) for k in (1, 2, 3)]
@@ -525,55 +547,75 @@
             copy.wait_recv()
         return buf[0] + buf[1] + buf[2] + buf[3]
 
-    for i in range(4):
-        relate_a(i)
-    m_sd.wait_recv()
-    m_sn.wait_recv()
+    teacher_a(0)
+    teacher_b(0)
+    student_b(0)
+    for j in range(4):
+        turn_own(j)
+    relate_a(0)
+    settle(2)
+    teacher_b(1)
+    student_b(1)
     relate_b(0)
-    finish(0); finish(4); go(m_ho[0])
-    relate_b(1)
-    finish(1); finish(5); go(m_ho[1])
+    finish(0)
+    teacher_a(1)
+    relate_a(1)
     chunk(0)
     p_ring[0].open()
-    relate_b(2)
-    finish(2); finish(6); go(m_ho[2])
+    settle(3)
+    relate_b(1)
+    finish(1)
+    teacher_b(2)
+    student_b(2)
+    p_ring[0].middle()
+    teacher_a(2)
+    relate_a(2)
     chunk(1)
     p_ring[1].open()
-    relate_b(3)
-    finish(3); finish(7); go(m_ho[3])
-    p_ring[0].middle()
+    relate_b(2)
+    finish(2)
+    teacher_b(3)
+    student_b(3)
+    to_q(0)
+    teacher_a(3)
+    relate_a(3)
     chunk(2)
     p_ring[2].open()
+    p_ring[1].middle()
+    q_ring[0].middle()
+    relate_b(3)
+    finish(3)
+    to_pair(0)
+    p_ring[2].middle()
+    to_q(1)
+    chunk(3)
+    p_ring[3].open()
+    pass_on(0)
     loss = losses[0]
     for part in losses[1:]:
         loss = loss + part
     loss = jnp.sum(loss, keepdims=True) * (1.0 / HEADS)
     lx[x] = jnp.broadcast_to(loss, (8, 128))
     c_x = spread(lx, x, on_x)
-    p_ring[1].middle()
-    chunk(3)
-    p_ring[3].open()
-    to_q(0)
-    p_ring[2].middle()
+    q_ring[1].middle()
+    to_q(2)
+    p_ring[3].middle()
+    to_pair(1)
+    q_ring[2].middle()
+    pass_on(1)
+    to_q(3)
     ly[y] = gathered(c_x, lx)
     c_y = spread(ly, y, on_y)
-    to_q(1)
-    q_ring[0].middle()
-    p_ring[3].middle()
-    to_q(2)
-    q_ring[1].middle()
+    to_pair(2)
+    total(0)
+    pass_on(2)
+    q_ring[3].middle()
     lz[zl] = gathered(c_y, ly)
     c_z = spread(lz, zl, on_zl)
-    to_pair(0)
-    to_q(3)
-    q_ring[2].middle()
-    to_pair(1)
-    total(0)
-    q_ring[3].middle()
-    to_pair(2)
     total(1)
     emit(0)
     to_pair(3)
+    pass_on(3)
     loss_out[...] = gathered(c_z, lz)
     total(2)
     emit(1)
@@ -598,21 +640,21 @@
     scratch += [b(8, 256, 256)] + [b(4, 256, 256)] * 8 + [b(8, 256, 256), b(2, 4, 256, 256)]
     scratch += [b(8, 256, 128), b(4, 256, 128), b(2, 4, 256, 128), b(8, 128, 256), b(2, 4, 128, 256)]
     scratch += [f(256, 256)] * 3 + [f(8, 2, 256, 256), f(8, 256), f(4, 2, 256, 256)]
-    scratch += [f(16, 256)] * 4
-    scratch += [f(8, 128, 256), b(8, 128, 256), b(8, 128, 256), b(4, 128, 256)]
+    scratch += [f(4, 4, 256)] * 4
+    scratch += [f(8, 128, 256)] + [b(8, 128, 256)] * 3 + [b(4, 128, 256)]
     scratch += [b(4, 4, 4, 128, 256)] + [b(4, 2, 128, 256)] * 6
     scratch += [b(4, 4, 128, 256)] + [b(4, 64, 256)] * 6
-    scratch += [b(4, 128, 256)] * 2 + [f(4, 128, 256)] * 2
+    scratch += [b(4, 128, 256)] * 3 + [f(4, 128, 256)] * 2
     scratch += [f(4, 8, 128)] * 3
     scratch += [
         pltpu.SemaphoreType.DMA((N_SEM,)), pltpu.SemaphoreType.DMA((N_SEM,)),
         pltpu.SemaphoreType.DMA((24,)),
     ]
-    ht, gt, loss = pl.pallas_call(
+    hidden_grad, wo_grad, loss = pl.pallas_call(
         kernel,
         out_shape=(
-            jax.ShapeDtypeStruct((1024, 256), BF16),
-            jax.ShapeDtypeStruct((1024, 256), F32),
+            jax.ShapeDtypeStruct((256, 1024), BF16),
+            jax.ShapeDtypeStruct((256, 1024), F32),
             jax.ShapeDtypeStruct((8, 128), F32),
         ),
         in_specs=[anywhere, anywhere, anywhere, vmem, pl.BlockSpec(memory_space=pltpu.SMEM)],
@@ -623,8 +665,8 @@
             collective_id=0, has_side_effects=True, vmem_limit_bytes=60 * 2**20
         ),
     )(teacher_part[0, 0], student_in[0], out_proj, segment_ids, valid_count)
-    state_grad = (ht.T.astype(F32) * UNSCALE)[None]
-    return (loss[0, :1], gt.T, state_grad)
+    state_grad = (hidden_grad.astype(F32) * UNSCALE)[None]
+    return (loss[0, :1], wo_grad, state_grad)
 
 
 def solution(mesh):

time: 138 us -> 141 us (1.022)
  the two profiles are of different devices: /device:TPU:9 before, /device:TPU:3 now
where the time goes in v2:
time: 141 us; the launch traced here: 140 us
  Pallas kernels  133 us (94%)
  local copies, waits for them, and re-layouts  3.5 us (2%)
  other arithmetic  2.13 us (2%)
    pallas_call x1, Pallas kernels, per_device(): pl.pallas_call(kernel, out_shape=(jax.ShapeDtypeStruct((256, 1024), BF16)...  133 us

profile of v2, /device:TPU:3, one launch (start us, length us, event | category | flops | bytes accessed | tf_op | source)
XLA Modules:
  0.0 140.4 jit_solution(5829778003644666411)
XLA Ops:
  1.3 133.4 %relation_step.1 = (bf16[256,1024]{1,0:T(8,128)(2,1)}, f32[256,1024]{1,0:T(8,128)}, f32[8,128]{1,0:T(8,128)}) custom-call(bf16[256,8192]{1,0:T(8,128)(2,1)} %bitcast.5, bf16[256,4096]{1,0:T(8,128)(2,1)} %bitcast.6, bf16[256,1024]{1,0:T(8,128)(2,1)} %win.1, s32[1,4096]{1,0:T(1,128)} %seg_ref.1, s32[1]{0:T(128)S(6)} %copy.9.valid_ref), custom_call_target="tpu_custom_call" | custom-call | tf_op jit(solution)/shard_map/relation_step/pallas_call | solution.py:653
  134.7 1.2 slice.3
  135.9 2.1 %multiply_bitcast_fusion = f32[1,256,1024]{2,1,0:T(8,128)} fusion(bf16[256,1024]{1,0:T(8,128)(2,1)} %get-tuple-element.8), kind=kLoop, calls=%fused_computation | loop fusion | flops 524288 | bytes 1572864 | tf_op jit(solution)/shard_map/broadcast_in_dim | solution.py:668
  138.1 2.3 %copy.10 = f32[256,1024]{1,0:T(8,128)} copy(f32[256,1024]{1,0:T(8,128)} %get-tuple-element.13) | data formatting | bytes 2097152

commit v3 on v2

--- a/solution.py
+++ b/solution.py
@@ -461,8 +461,11 @@
         def at(self, k, half):
             return self.unit.at[(self.me + k) % 4].at[half]
 
-        def open(self):
-            go(self.s1p); go(self.s1m); go(self.dp); go(self.dm)
+        def far(self):
+            go(self.s1p); go(self.s1m)
+
+        def near(self):
+            go(self.dp); go(self.dm)
 
         def middle(self):
             lo, hi = self.halves
@@ -516,7 +519,8 @@
 
     def to_q(j):
         p_ring[j].close(qb.at[j])
-        q_ring[j].open()
+        q_ring[j].far()
+        q_ring[j].near()
 
     def to_pair(j):
         q_ring[j].close(fin.at[j])
@@ -547,87 +551,97 @@
             copy.wait_recv()
         return buf[0] + buf[1] + buf[2] + buf[3]
 
+    settle(2)
     teacher_a(0)
     teacher_b(0)
     student_b(0)
+    teacher_b(1)
+    student_b(1)
     for j in range(4):
         turn_own(j)
     relate_a(0)
-    settle(2)
-    teacher_b(1)
-    student_b(1)
-    relate_b(0)
-    finish(0)
     teacher_a(1)
     relate_a(1)
-    chunk(0)
-    p_ring[0].open()
-    settle(3)
+    relate_b(0)
     relate_b(1)
-    finish(1)
     teacher_b(2)
     student_b(2)
-    p_ring[0].middle()
+    settle(3)
     teacher_a(2)
     relate_a(2)
-    chunk(1)
-    p_ring[1].open()
+    finish(0)
     relate_b(2)
-    finish(2)
+    finish(1)
     teacher_b(3)
     student_b(3)
-    to_q(0)
     teacher_a(3)
     relate_a(3)
+    chunk(0)
+    p_ring[0].far()
+    finish(2)
+    chunk(1)
+    p_ring[1].far()
+    p_ring[1].near()
+    relate_b(3)
+    p_ring[0].near()
     chunk(2)
-    p_ring[2].open()
-    p_ring[1].middle()
-    q_ring[0].middle()
-    relate_b(3)
-    finish(3)
-    to_pair(0)
-    p_ring[2].middle()
-    to_q(1)
-    chunk(3)
-    p_ring[3].open()
-    pass_on(0)
+    p_ring[2].far()
     loss = losses[0]
     for part in losses[1:]:
         loss = loss + part
     loss = jnp.sum(loss, keepdims=True) * (1.0 / HEADS)
     lx[x] = jnp.broadcast_to(loss, (8, 128))
     c_x = spread(lx, x, on_x)
+    p_ring[0].middle()
+    p_ring[2].near()
+    finish(3)
+    chunk(3)
+    p_ring[3].far()
+    p_ring[1].middle()
+    p_ring[2].middle()
+    p_ring[3].near()
+    to_q(0)
+    to_q(1)
+    p_ring[3].middle()
+    ly[y] = gathered(c_x, lx)
+    c_y = spread(ly, y, on_y)
+    q_ring[0].middle()
     q_ring[1].middle()
     to_q(2)
-    p_ring[3].middle()
+    to_pair(0)
     to_pair(1)
     q_ring[2].middle()
+    pass_on(0)
     pass_on(1)
     to_q(3)
-    ly[y] = gathered(c_x, lx)
-    c_y = spread(ly, y, on_y)
     to_pair(2)
-    total(0)
-    pass_on(2)
-    q_ring[3].middle()
     lz[zl] = gathered(c_y, ly)
     c_z = spread(lz, zl, on_zl)
+    q_ring[3].middle()
+    pass_on(2)
+    total(0)
     total(1)
     emit(0)
     to_pair(3)
+    emit(1)
+    total(2)
     pass_on(3)
+    emit(2)
     loss_out[...] = gathered(c_z, lz)
-    total(2)
-    emit(1)
     total(3)
-    emit(2)
     emit(3)
     for copy in pending:
         copy.wait_send()
 
 
+def results(h_ref, g_ref, l_ref, loss_ref, wo_ref, state_ref):
+    loss_ref[0] = jnp.max(l_ref[0:1, 0:1])
+    wo_ref[...] = g_ref[...]
+    state_ref[...] = h_ref[...].astype(F32) * UNSCALE
+
+
 def per_device(teacher_part, student_in, out_proj, segment_ids, valid_count):
-    anywhere = pl.BlockSpec(memory_space=pl.ANY)
+    anywhere = pl.BlockSpec(memory_space=pltpu.HBM)
     vmem = pl.BlockSpec(memory_space=pltpu.VMEM)
 
     def b(*shape):
@@ -665,8 +679,19 @@
             collective_id=0, has_side_effects=True, vmem_limit_bytes=60 * 2**20
         ),
     )(teacher_part[0, 0], student_in[0], out_proj, segment_ids, valid_count)
-    state_grad = (hidden_grad.astype(F32) * UNSCALE)[None]
-    return (loss[0, :1], wo_grad, state_grad)
+    doc_loss, wo_grad, state_grad = pl.pallas_call(
+        results,
+        out_shape=(
+            jax.ShapeDtypeStruct((1,), F32),
+            jax.ShapeDtypeStruct((256, 1024), F32),
+            jax.ShapeDtypeStruct((256, 1024), F32),
+        ),
+        in_specs=[vmem, vmem, vmem],
+        out_specs=(pl.BlockSpec(memory_space=pltpu.SMEM), vmem, vmem),
+        name="results",
+        compiler_params=pltpu.CompilerParams(vmem_limit_bytes=16 * 2**20),
+    )(hidden_grad, wo_grad, loss)
+    return (doc_loss, wo_grad, state_grad[None])
 
 
 def solution(mesh):

time: 141 us -> 133 us (0.943)
  Pallas kernels: 133 us -> 127 us
  other arithmetic: 2.13 us -> 0 us
    pallas_call x1, Pallas kernels: 133 us -> 125 us  [per_device(): pl.pallas_call(kernel, out_shape=(jax.ShapeDtypeStruct((256, 1024), BF16)...]
    broadcast_in_dim x1 -> x0, other arithmetic: 2.13 us -> none  [per_device(): state_grad = (hidden_grad.astype(F32) * UNSCALE)[None]]
    unnamed x1 -> x6, local copies, waits for them, and re-layouts: 2.31 us -> 2.94 us
where the time goes in v3:
time: 133 us; the launch traced here: 131 us
  Pallas kernels  127 us (95%)
  local copies, waits for them, and re-layouts  2.94 us (2%)
  between operations  1.46 us (1%)
    pallas_call x1, Pallas kernels, per_device(): pl.pallas_call(kernel, out_shape=(jax.ShapeDtypeStruct((256, 1024), BF16)...  125 us
    unnamed x6, local copies, waits for them, and re-layouts  2.94 us

profile of v3, /device:TPU:3, one launch (start us, length us, event | category | flops | bytes accessed | tf_op | source)
XLA Modules:
  0.0 131.2 jit_solution(8332735592292141357)
XLA Ops:
  1.3 125.4 %relation_step.1 = (bf16[256,1024]{1,0:T(8,128)(2,1)}, f32[256,1024]{1,0:T(8,128)}, f32[8,128]{1,0:T(8,128)}) custom-call(bf16[256,8192]{1,0:T(8,128)(2,1)} %bitcast.3, bf16[256,4096]{1,0:T(8,128)(2,1)} %bitcast.4, bf16[256,1024]{1,0:T(8,128)(2,1)} %win.1, s32[1,4096]{1,0:T(1,128)} %seg_ref.1, s32[1]{0:T(128)S(6)} %copy.8.valid_ref), custom_call_target="tpu_custom_call" | custom-call | tf_op jit(solution)/shard_map/relation_step/pallas_call | solution.py:667
  126.7 0.0 copy-start
  126.7 1.2 copy-done
  127.9 0.0 copy-start.1
  127.9 1.0 copy-done.1
  128.9 0.0 copy-start.2
  128.9 0.7 copy-done.2
  129.6 1.4 %results.1 = (f32[1]{0:T(128)}, f32[256,1024]{1,0:T(8,128)}, f32[256,1024]{1,0:T(8,128)}) custom-call(bf16[256,1024]{1,0:T(8,128)(2,1)S(1)} %copy-done.1, f32[256,1024]{1,0:T(8,128)S(1)} %copy-done, f32[8,128]{1,0:T(8,128)S(1)} %copy-done.2), custom_call_target="tpu_custom_call" | custom-call | tf_op jit(solution)/shard_map/results/pallas_call | solution.py:682
Async XLA Ops:
  126.7 1.2 copy-start
  127.9 1.0 copy-start.1
  128.9 0.7 copy-start.2

commit v4 on v3

--- a/solution.py
+++ b/solution.py
@@ -426,7 +426,7 @@
         h_out[:, j * 128:(j + 1) * 128] = turned(low)
         h_out[:, (4 + j) * 128:(5 + j) * 128] = turned(high)
 
-    first_y = [True, False, True, True]
+    first_y = [False, True, True, True]
 
     def chunk(j):
         m_ho[j].wait_recv()
@@ -566,24 +566,25 @@
     relate_b(1)
     teacher_b(2)
     student_b(2)
+    finish(0)
     settle(3)
     teacher_a(2)
     relate_a(2)
-    finish(0)
     relate_b(2)
+    chunk(0)
+    p_ring[0].far()
+    p_ring[0].near()
     finish(1)
     teacher_b(3)
     student_b(3)
     teacher_a(3)
     relate_a(3)
-    chunk(0)
-    p_ring[0].far()
-    finish(2)
     chunk(1)
     p_ring[1].far()
+    finish(2)
+    p_ring[0].middle()
+    relate_b(3)
     p_ring[1].near()
-    relate_b(3)
-    p_ring[0].near()
     chunk(2)
     p_ring[2].far()
     loss = losses[0]
@@ -592,42 +593,41 @@
     loss = jnp.sum(loss, keepdims=True) * (1.0 / HEADS)
     lx[x] = jnp.broadcast_to(loss, (8, 128))
     c_x = spread(lx, x, on_x)
-    p_ring[0].middle()
+    p_ring[1].middle()
     p_ring[2].near()
     finish(3)
     chunk(3)
     p_ring[3].far()
-    p_ring[1].middle()
+    to_q(0)
     p_ring[2].middle()
     p_ring[3].near()
-    to_q(0)
     to_q(1)
-    p_ring[3].middle()
     ly[y] = gathered(c_x, lx)
     c_y = spread(ly, y, on_y)
     q_ring[0].middle()
+    p_ring[3].middle()
     q_ring[1].middle()
-    to_q(2)
     to_pair(0)
     to_pair(1)
+    to_q(2)
+    pass_on(0)
+    lz[zl] = gathered(c_y, ly)
+    c_z = spread(lz, zl, on_zl)
     q_ring[2].middle()
-    pass_on(0)
     pass_on(1)
     to_q(3)
     to_pair(2)
-    lz[zl] = gathered(c_y, ly)
-    c_z = spread(lz, zl, on_zl)
+    total(0)
     q_ring[3].middle()
     pass_on(2)
-    total(0)
     total(1)
     emit(0)
     to_pair(3)
     emit(1)
+    loss_out[...] = gathered(c_z, lz)
     total(2)
     pass_on(3)
     emit(2)
-    loss_out[...] = gathered(c_z, lz)
     total(3)
     emit(3)
     for copy in pending:

time: 133 us -> 136 us (1.023)
  Pallas kernels: 127 us -> 129 us
    pallas_call x1, Pallas kernels: 125 us -> 128 us  [per_device(): pl.pallas_call(kernel, out_shape=(jax.ShapeDtypeStruct((256, 1024), BF16)...]
where the time goes in v4:
time: 136 us; the launch traced here: 134 us
  Pallas kernels  129 us (95%)
  local copies, waits for them, and re-layouts  2.94 us (2%)
  between operations  1.46 us (1%)
    pallas_call x1, Pallas kernels, per_device(): pl.pallas_call(kernel, out_shape=(jax.ShapeDtypeStruct((256, 1024), BF16)...  128 us
    unnamed x6, local copies, waits for them, and re-layouts  2.94 us

profile of v4, /device:TPU:3, one launch (start us, length us, event | category | flops | bytes accessed | tf_op | source)
XLA Modules:
  0.0 133.8 jit_solution(15777612652297412028)
XLA Ops:
  1.3 128.0 %relation_step.1 = (bf16[256,1024]{1,0:T(8,128)(2,1)}, f32[256,1024]{1,0:T(8,128)}, f32[8,128]{1,0:T(8,128)}) custom-call(bf16[256,8192]{1,0:T(8,128)(2,1)} %bitcast.3, bf16[256,4096]{1,0:T(8,128)(2,1)} %bitcast.4, bf16[256,1024]{1,0:T(8,128)(2,1)} %win.1, s32[1,4096]{1,0:T(1,128)} %seg_ref.1, s32[1]{0:T(128)S(6)} %copy.8.valid_ref), custom_call_target="tpu_custom_call" | custom-call | tf_op jit(solution)/shard_map/relation_step/pallas_call | solution.py:667
  129.3 0.0 copy-start
  129.3 1.2 copy-done
  130.5 0.0 copy-start.1
  130.6 1.0 copy-done.1
  131.6 0.0 copy-start.2
  131.6 0.7 copy-done.2
  132.3 1.4 %results.1 = (f32[1]{0:T(128)}, f32[256,1024]{1,0:T(8,128)}, f32[256,1024]{1,0:T(8,128)}) custom-call(bf16[256,1024]{1,0:T(8,128)(2,1)S(1)} %copy-done.1, f32[256,1024]{1,0:T(8,128)S(1)} %copy-done, f32[8,128]{1,0:T(8,128)S(1)} %copy-done.2), custom_call_target="tpu_custom_call" | custom-call | tf_op jit(solution)/shard_map/results/pallas_call | solution.py:682
Async XLA Ops:
  129.3 1.2 copy-start
  130.5 1.0 copy-start.1
  131.6 0.7 copy-start.2

commit v5 on v3

--- a/solution.py
+++ b/solution.py
@@ -32,6 +32,10 @@
     return jnp.transpose(a.astype(F32)).astype(BF16)
 
 
+def neutral_rows():
+    return jnp.where(lax.broadcasted_iota(jnp.int32, (4, 256), 0) % 2 == 0, NEG, 0.0).astype(F32)
+
+
 def kernel(
     tpart, xin, win, seg_ref, valid_ref,
     h_out, gt_out, loss_out,
@@ -40,7 +44,7 @@
     ss, so, sx, st, sxt,
     mo, mp, mn, zt, lt, zs, st_d, st_n, rs_d, rs_n,
     hacc, hsend, hrecv, ht, ho,
-    gb, p1p, p1m, pdp, pdm, p2p, p2m, qb, q1p, q1m, qdp, qdm, q2p, q2m, fin, fin_m, fin_r, gf, gf_r,
+    gb, p1p, p1m, pdp, pdm, p2p, p2m, qb, q1p, q1m, qdp, qdm, q2p, q2m, fin, fin_r, gf, gf_r,
     lx, ly, lz,
     send_sem, recv_sem, loc_sem,
 ):
@@ -85,6 +89,37 @@
         copy.start()
         pending.append(copy)
         return copy
+
+    has_next, has_prev = ctx < 15, ctx > 0
+    guarded = []
+
+    def go_if(cond, copy):
+        guarded.append((cond, copy))
+
+        @pl.when(cond)
+        def _():
+            copy.start()
+
+    def recv_if(cond, copy):
+        @pl.when(cond)
+        def _():
+            copy.wait_recv()
+
+    @pl.when(ctx == 0)
+    def _():
+        tx[0] = jnp.zeros_like(tx[0])
+        sx[0] = jnp.zeros_like(sx[0])
+        for i in range(4):
+            rs_n[i] = neutral_rows()
+            hrecv[4 + i] = jnp.zeros_like(hrecv[4 + i])
+
+    @pl.when(ctx == 15)
+    def _():
+        tx[1] = jnp.zeros_like(tx[1])
+        sx[1] = jnp.zeros_like(sx[1])
+        for i in range(4):
+            rs_d[i] = neutral_rows()
+            hrecv[i] = jnp.zeros_like(hrecv[i])
 
     locs = [0]
 
@@ -225,14 +260,14 @@
         m_dm[i].wait_recv()
         own_loc[i].wait()
         tt[i] = (t_own[i].astype(F32) + r2p[i].astype(F32) + rdm[i].astype(F32)).astype(BF16)
-        go(m_ta[i])
+        go_if(has_next, m_ta[i])
         m_s2m[i].wait_recv()
         m_dp[i].wait_recv()
         own_loc[4 + i].wait()
         tt[4 + i] = (
             t_own[4 + i].astype(F32) + r2m[i].astype(F32) + rdp[i].astype(F32)
         ).astype(BF16)
-        go(m_tb[i])
+        go_if(has_prev, m_tb[i])
 
     ag_wait(0, 1)
     ag_start(4, 5, 6, 7, 8, 9)
@@ -301,15 +336,15 @@
     go(m_so)
     for j in range(4):
         ss[core * 4 + j] = acc_own[:, j * 128:(j + 1) * 128]
-        go(half_copy(core, j))
+        go_if(core * ctx + other * (15 - ctx) > 0, half_copy(core, j))
     for j in range(4):
         st[core * 4 + j] = turned(acc_own[:, j * 128:(j + 1) * 128])
     m_so.wait_recv()
     for j in range(4):
-        go(half_copy(other, j))
+        go_if(other * ctx + core * (15 - ctx) > 0, half_copy(other, j))
 
     def teacher_a(i):
-        m_ta[i].wait_recv()
+        recv_if(has_prev, m_ta[i])
         q = tt[i]
         own = dot_nt(q, q) * T_SCALE + mo[...]
         off = dot_nt(tx[0, i], q) * T_SCALE + mp[...]
@@ -333,7 +368,7 @@
         return own, off
 
     def teacher_b(i):
-        m_tb[i].wait_recv()
+        recv_if(has_next, m_tb[i])
         k = tt[4 + i]
         own = dot_nt(k, k) * T_SCALE + mo[...]
         off = dot_nt(k, tx[1, i]) * T_SCALE + mn[...]
@@ -343,13 +378,13 @@
     m_sn = [remote(st_n.at[i], rs_n.at[i], nxt) for i in range(4)]
 
     def student_b(i):
-        half_copy(1, i).wait_recv()
+        recv_if(has_next, half_copy(1, i))
         k = ss[4 + i]
         own = dot_nt(k, k) * S_SCALE + mo[...]
         off = dot_nt(k, sx[1, i]) * S_SCALE + mn[...]
         zs[i, 0], zs[i, 1] = b_stats(own, off, i, 2)
-        go(m_sd[i])
-        go(m_sn[i])
+        go_if(has_prev, m_sd[i])
+        go_if(has_next, m_sn[i])
         sxt[1, i] = turned(sx[1, i])
 
     def turn_own(j):
@@ -368,7 +403,7 @@
     losses = []
 
     def relate_a(i):
-        half_copy(0, i).wait_recv()
+        recv_if(has_prev, half_copy(0, i))
         sxt[0, i] = turned(sx[0, i])
         q = ss[i]
         own = dot_nt(q, q) * S_SCALE + mo[...]
@@ -384,7 +419,7 @@
         losses.append(loss_o + loss_p)
         turned_q = st[i]
         hsend[i] = dot_nt(turned_q, g_off).astype(BF16)
-        go(m_h[i])
+        go_if(has_prev, m_h[i])
         hacc[i] = dot_nn(sxt[0, i], g_off) + dot_nn(turned_q, g_own) + dot_nt(turned_q, g_own)
 
     def shifts(m_here, l_here, m_there, l_there):
@@ -393,8 +428,8 @@
         return (m_here - top) - jnp.log(total)
 
     def relate_b(i):
-        m_sd[i].wait_recv()
-        m_sn[i].wait_recv()
+        recv_if(has_next, m_sd[i])
+        recv_if(has_prev, m_sn[i])
 
         def row(ref, r):
             return ref[i, r:r + 1]
@@ -408,11 +443,11 @@
         losses.append(loss_o + loss_n)
         turned_k = st[4 + i]
         hsend[4 + i] = dot_nn(turned_k, g_off).astype(BF16)
-        go(m_h[4 + i])
+        go_if(has_next, m_h[4 + i])
         hacc[4 + i] = dot_nn(turned_k, g_own) + dot_nt(turned_k, g_own) + dot_nt(sxt[1, i], g_off)
 
     def finish_one(i):
-        m_h[i].wait_recv()
+        recv_if(has_next if i < 4 else has_prev, m_h[i])
         full = (hacc[i] + hrecv[i].astype(F32)).astype(BF16)
         ht[i] = full
         return full
@@ -504,17 +539,7 @@
              (pl.ds(0, 64), pl.ds(64, 64)))
         for j in range(4)
     ]
-    low, high = pl.ds(0, 64), pl.ds(64, 64)
-    m_f1 = [
-        (remote(fin.at[j, low], fin_m.at[j, low], on_z(2)),
-         remote(fin.at[j, high], fin_m.at[j, high], on_z(6)))
-        for j in range(4)
-    ]
-    m_f2 = [
-        (remote(fin_m.at[j, low], fin_r.at[j, low], on_z(2)),
-         remote(fin_m.at[j, high], fin_r.at[j, high], on_z(6)))
-        for j in range(4)
-    ]
+    m_fin = [remote(fin.at[j], fin_r.at[j], on_z(4)) for j in range(4)]
     m_gf = [remote(gf.at[j], gf_r.at[j], mate) for j in range(4)]
 
     def to_q(j):
@@ -524,17 +549,10 @@
 
     def to_pair(j):
         q_ring[j].close(fin.at[j])
-        for copy in m_f1[j]:
-            go(copy)
-
-    def pass_on(j):
-        for come, leave in zip(m_f1[j], m_f2[j]):
-            come.wait_recv()
-            go(leave)
+        go(m_fin[j])
 
     def total(j):
-        for copy in m_f2[j]:
-            copy.wait_recv()
+        m_fin[j].wait_recv()
         gf[j] = fin[j].astype(F32) + fin_r[j].astype(F32)
         go(m_gf[j])
         gt_out[:, pl.ds(pl.multiple_of(core * 512 + j * 128, 128), 128)] = jnp.transpose(gf[j])
@@ -611,27 +629,28 @@
     to_pair(0)
     to_pair(1)
     q_ring[2].middle()
-    pass_on(0)
-    pass_on(1)
     to_q(3)
     to_pair(2)
     lz[zl] = gathered(c_y, ly)
     c_z = spread(lz, zl, on_zl)
     q_ring[3].middle()
-    pass_on(2)
     total(0)
     total(1)
     emit(0)
     to_pair(3)
     emit(1)
     total(2)
-    pass_on(3)
     emit(2)
     loss_out[...] = gathered(c_z, lz)
     total(3)
     emit(3)
     for copy in pending:
         copy.wait_send()
+    for cond, copy in guarded:
+
+        @pl.when(cond)
+        def _():
+            copy.wait_send()
 
 
 def results(h_ref, g_ref, l_ref, loss_ref, wo_ref, state_ref):
@@ -658,7 +677,7 @@
     scratch += [f(8, 128, 256)] + [b(8, 128, 256)] * 3 + [b(4, 128, 256)]
     scratch += [b(4, 4, 4, 128, 256)] + [b(4, 2, 128, 256)] * 6
     scratch += [b(4, 4, 128, 256)] + [b(4, 64, 256)] * 6
-    scratch += [b(4, 128, 256)] * 3 + [f(4, 128, 256)] * 2
+    scratch += [b(4, 128, 256)] * 2 + [f(4, 128, 256)] * 2
     scratch += [f(4, 8, 128)] * 3
     scratch += [
         pltpu.SemaphoreType.DMA((N_SEM,)), pltpu.SemaphoreType.DMA((N_SEM,)),

time: 133 us -> 127 us (0.955)
  the two profiles are of different devices: /device:TPU:3 before, /device:TPU:39 now
where the time goes in v5:
time: 127 us
  Pallas kernels  122 us (96%)
  local copies, waits for them, and re-layouts  2.94 us (2%)
  between operations  1.46 us (1%)
    pallas_call x1, Pallas kernels, per_device(): pl.pallas_call(kernel, out_shape=(jax.ShapeDtypeStruct((256, 1024), BF16)...  121 us
    unnamed x6, local copies, waits for them, and re-layouts  2.94 us

profile of v5, /device:TPU:39, one launch (start us, length us, event | category | flops | bytes accessed | tf_op | source)
XLA Modules:
  0.0 126.7 jit_solution(3149017693949951717)
XLA Ops:
  1.3 120.8 %relation_step.1 = (bf16[256,1024]{1,0:T(8,128)(2,1)}, f32[256,1024]{1,0:T(8,128)}, f32[8,128]{1,0:T(8,128)}) custom-call(bf16[256,8192]{1,0:T(8,128)(2,1)} %bitcast.3, bf16[256,4096]{1,0:T(8,128)(2,1)} %bitcast.4, bf16[256,1024]{1,0:T(8,128)(2,1)} %win.1, s32[1,4096]{1,0:T(1,128)} %seg_ref.1, s32[1]{0:T(128)S(6)} %copy.8.valid_ref), custom_call_target="tpu_custom_call" | custom-call | tf_op jit(solution)/shard_map/relation_step/pallas_call | solution.py:686
  122.1 0.0 copy-start
  122.1 1.2 copy-done
  123.4 0.0 copy-start.1
  123.4 1.0 copy-done.1
  124.4 0.0 copy-start.2
  124.4 0.7 copy-done.2
  125.1 1.4 %results.1 = (f32[1]{0:T(128)}, f32[256,1024]{1,0:T(8,128)}, f32[256,1024]{1,0:T(8,128)}) custom-call(bf16[256,1024]{1,0:T(8,128)(2,1)S(1)} %copy-done.1, f32[256,1024]{1,0:T(8,128)S(1)} %copy-done, f32[8,128]{1,0:T(8,128)S(1)} %copy-done.2), custom_call_target="tpu_custom_call" | custom-call | tf_op jit(solution)/shard_map/results/pallas_call | solution.py:701
Async XLA Ops:
  122.1 1.2 copy-start
  123.4 1.0 copy-start.1
  124.4 0.7 copy-start.2

commit v6 on v5

--- a/solution.py
+++ b/solution.py
@@ -160,7 +160,7 @@
         return ((zl + dz) % 4) * 4 + (y + dy) % 4
 
     def gather_messages(kind):
-        base = kind * 128
+        base, rows = ((0, 96), (96, 160))[kind]
 
         def at(dp_, dq_):
             return block(dq_, dp_) if kind == 0 else block(dp_, dq_)
@@ -171,7 +171,7 @@
             return on_z(k % 8) if on_z_axis else on_y(k % 4)
 
         def piece(dp_, dq_, part):
-            start, size = {"all": (0, 128), "lo": (0, 64), "hi": (64, 64)}[part]
+            start, size = {"all": (0, rows), "lo": (0, rows // 2), "hi": (rows // 2, rows // 2)}[part]
             b = at(dp_, dq_)
             return wb.at[b, pl.ds(base + start, size)]
 
@@ -179,7 +179,7 @@
             ref = piece(dp_, dq_, part)
             return remote(ref, ref, to(which, sign))
 
-        own = win.at[pl.ds(base, 128), pl.ds(col0, 512)]
+        own = win.at[pl.ds(base, rows), pl.ds(col0, 512)]
 
         def first(which, sign):
             return remote(own, piece(0, 0, "all"), to(which, sign))

time: 127 us -> 123 us (0.969)
  the two profiles are of different devices: /device:TPU:39 before, /device:TPU:3 now
where the time goes in v6:
time: 123 us; the launch traced here: 122 us
  Pallas kernels  118 us (96%)
  local copies, waits for them, and re-layouts  2.94 us (2%)
  between operations  1.46 us (1%)
    pallas_call x1, Pallas kernels, per_device(): pl.pallas_call(kernel, out_shape=(jax.ShapeDtypeStruct((256, 1024), BF16)...  116 us
    unnamed x6, local copies, waits for them, and re-layouts  2.94 us

profile of v6, /device:TPU:3, one launch (start us, length us, event | category | flops | bytes accessed | tf_op | source)
XLA Modules:
  0.0 122.3 jit_solution(9173562115482357994)
XLA Ops:
  1.3 116.5 %relation_step.1 = (bf16[256,1024]{1,0:T(8,128)(2,1)}, f32[256,1024]{1,0:T(8,128)}, f32[8,128]{1,0:T(8,128)}) custom-call(bf16[256,8192]{1,0:T(8,128)(2,1)} %bitcast.3, bf16[256,4096]{1,0:T(8,128)(2,1)} %bitcast.4, bf16[256,1024]{1,0:T(8,128)(2,1)} %win.1, s32[1,4096]{1,0:T(1,128)} %seg_ref.1, s32[1]{0:T(128)S(6)} %copy.8.valid_ref), custom_call_target="tpu_custom_call" | custom-call | tf_op jit(solution)/shard_map/relation_step/pallas_call | solution.py:686
  117.7 0.0 copy-start
  117.8 1.2 copy-done
  119.0 0.0 copy-start.1
  119.0 1.0 copy-done.1
  120.0 0.0 copy-start.2
  120.0 0.7 copy-done.2
  120.7 1.4 %results.1 = (f32[1]{0:T(128)}, f32[256,1024]{1,0:T(8,128)}, f32[256,1024]{1,0:T(8,128)}) custom-call(bf16[256,1024]{1,0:T(8,128)(2,1)S(1)} %copy-done.1, f32[256,1024]{1,0:T(8,128)S(1)} %copy-done, f32[8,128]{1,0:T(8,128)S(1)} %copy-done.2), custom_call_target="tpu_custom_call" | custom-call | tf_op jit(solution)/shard_map/results/pallas_call | solution.py:701
Async XLA Ops:
  117.7 1.2 %copy-start = (f32[256,1024]{1,0:T(8,128)S(1)}, f32[256,1024]{1,0:T(8,128)}, u32[]{:S(2)}) copy-start(f32[256,1024]{1,0:T(8,128)} %get-tuple-element.10.g_ref) | copy-start | bytes 3145732
  119.0 1.0 copy-start.1
  120.0 0.7 copy-start.2

commit v7 on v6

--- a/solution.py
+++ b/solution.py
@@ -589,18 +589,18 @@
     relate_a(2)
     finish(0)
     relate_b(2)
+    chunk(0)
+    p_ring[0].far()
     finish(1)
     teacher_b(3)
     student_b(3)
     teacher_a(3)
     relate_a(3)
-    chunk(0)
-    p_ring[0].far()
     finish(2)
     chunk(1)
     p_ring[1].far()
+    relate_b(3)
     p_ring[1].near()
-    relate_b(3)
     p_ring[0].near()
     chunk(2)
     p_ring[2].far()
@@ -708,7 +708,7 @@
         in_specs=[vmem, vmem, vmem],
         out_specs=(pl.BlockSpec(memory_space=pltpu.SMEM), vmem, vmem),
         name="results",
-        compiler_params=pltpu.CompilerParams(vmem_limit_bytes=16 * 2**20),
+        compiler_params=pltpu.CompilerParams(vmem_limit_bytes=60 * 2**20),
     )(hidden_grad, wo_grad, loss)
     return (doc_loss, wo_grad, state_grad[None])
 

time: 123 us -> 121 us (0.984); the launches traced: 122 us -> 119 us
  local copies, waits for them, and re-layouts: 2.94 us -> 0 us
    unnamed x6 -> x0, local copies, waits for them, and re-layouts: 2.94 us -> none
    pallas_call x1, Pallas kernels: 116 us -> 115 us  [per_device(): pl.pallas_call(kernel, out_shape=(jax.ShapeDtypeStruct((256, 1024), BF16)...]
    pallas_call x1, Pallas kernels: 1.41 us -> 2.76 us  [per_device(): pl.pallas_call(results, out_shape=(jax.ShapeDtypeStruct((1,), F32), jax.S...]
where the time goes in v7:
time: 121 us; the launch traced here: 119 us
  Pallas kernels  118 us (98%)
  between operations  1.45 us (1%)
    pallas_call x1, Pallas kernels, per_device(): pl.pallas_call(kernel, out_shape=(jax.ShapeDtypeStruct((256, 1024), BF16)...  115 us
    pallas_call x1, Pallas kernels, per_device(): pl.pallas_call(results, out_shape=(jax.ShapeDtypeStruct((1,), F32), jax.S...  2.76 us

profile of v7, /device:TPU:3, one launch (start us, length us, event | category | flops | bytes accessed | tf_op | source)
XLA Modules:
  0.0 119.0 jit_solution(10812051290121758088)
XLA Ops:
  1.3 114.7 %relation_step.1 = (bf16[256,1024]{1,0:T(8,128)(2,1)}, f32[256,1024]{1,0:T(8,128)}, f32[8,128]{1,0:T(8,128)}) custom-call(bf16[256,8192]{1,0:T(8,128)(2,1)} %bitcast.3, bf16[256,4096]{1,0:T(8,128)(2,1)} %bitcast.4, bf16[256,1024]{1,0:T(8,128)(2,1)} %win.1, s32[1,4096]{1,0:T(1,128)} %seg_ref.1, s32[1]{0:T(128)S(6)} %copy.8.valid_ref), custom_call_target="tpu_custom_call" | custom-call | tf_op jit(solution)/shard_map/relation_step/pallas_call | solution.py:686
  116.0 2.8 %results.1 = (f32[1]{0:T(128)}, f32[256,1024]{1,0:T(8,128)}, f32[256,1024]{1,0:T(8,128)}) custom-call(bf16[256,1024]{1,0:T(8,128)(2,1)} %get-tuple-element.9.h_ref, f32[256,1024]{1,0:T(8,128)} %get-tuple-element.10.g_ref, f32[8,128]{1,0:T(8,128)} %get-tuple-element.11.l_ref), custom_call_target="tpu_custom_call" | custom-call | tf_op jit(solution)/shard_map/results/pallas_call | solution.py:701
